TPU v7x, 128 devices: a whole 4x4x4 slice. The times are simulated.
128 devices in a mesh: rows: 16 (over z, x), cols: 8 (over y, core).
Axes of the slice: x: 4, y: 4, z: 4, core: 2. Of those that a mesh axis runs over, the one named last changes fastest.
Arguments:
- points: float32 [160, 127], replicated, may hold values from -0.5 to 0.5
- noise: float32 [160, 128], replicated, may hold values from 0.3 to 3
- basis: float32 [20480, 128], P('rows'), may hold values from -0.5 to 0.5
Outputs:
- factor: float32 [20480, 20480], P('rows', 'cols')
All inputs are finite; a program needn't handle non-finite values.
Results may differ from a plain program's by a relative error of at most 0.0003.
Values sent between devices are 32-bit elements; how exact they have to be, the bound alone decides.
A program may use at most 128 MiB of HBM per device.

v0:
```python
import jax
import jax.numpy as jnp
from jax import lax
from jax.sharding import PartitionSpec as P

PW = 256
PANELS = 2
LEAD = 512


def from_root(x, axis, root):
    mine = lax.axis_index(axis) == root
    return lax.psum(jnp.where(mine, x, jnp.zeros_like(x)), axis)


def tile_rows(point_row, col_points):
    rho = point_row[None, :] - col_points
    kval = jnp.exp(-0.5 * jnp.sum(rho * rho, axis=1))
    ones = jnp.ones((col_points.shape[0], 1), jnp.float32)
    left = jnp.concatenate([ones, -rho], axis=1)
    right = jnp.concatenate([ones, rho], axis=1)
    width = left.shape[1]
    jmat = jnp.diag((jnp.arange(width) > 0).astype(jnp.float32))
    tiles = kval[None, :, None] * (jmat[:, None, :] + left.T[:, :, None] * right[None, :, :])
    return tiles.reshape(width, -1)


def point_rows(point_row, noise_row, basis_row, start, col_points, col_basis, col_start):
    width = noise_row.shape[0]
    values = tile_rows(point_row, col_points) + jnp.dot(
        basis_row, col_basis.T, precision=lax.Precision.HIGHEST
    )
    row_ids = start + jnp.arange(width)
    col_ids = col_start + jnp.arange(values.shape[1])
    same = row_ids[:, None] == col_ids[None, :]
    return values + jnp.where(same, noise_row[:, None], jnp.float32(0.0))


def assemble(points_rows, noise_rows, basis_rows, starts, col_points, col_basis, col_start):
    count, width = noise_rows.shape
    basis_split = basis_rows.reshape(count, width, -1)

    def assemble_single(items):
        return point_rows(items[0], items[1], items[2], items[3], col_points, col_basis, col_start)

    blocks = lax.map(assemble_single, (points_rows, noise_rows, basis_split, starts))
    return blocks.reshape(count * width, -1)


def mask_panel(panel, row_ids, low):
    col_ids = low + jnp.arange(panel.shape[1])
    return jnp.where(row_ids[:, None] < col_ids[None, :], jnp.float32(0.0), panel)


def finish(
    points_rows,
    noise_rows,
    basis_rows,
    starts,
    lead_rows,
    col_points,
    col_basis,
    col_start,
    lead_cols,
):
    count, width = noise_rows.shape
    ncols = lead_cols.shape[0]
    leading = lead_rows.shape[1]
    cross = lead_cols.T
    col_ids = col_start + jnp.arange(ncols)

    def finish_single(items):
        prow, nrow, brow, lrow, start = items
        values = point_rows(prow, nrow, brow, start, col_points, col_basis, col_start)
        trail = values - jnp.dot(lrow, cross, precision=lax.Precision.HIGHEST)
        row_ids = start + jnp.arange(width)
        own = jnp.pad(lrow, ((0, 0), (0, ncols - leading)))
        mirror = lax.dynamic_slice_in_dim(cross, jnp.minimum(start, leading - width), width, 0)
        inner = jnp.where(row_ids[:, None] < leading, mirror, trail)
        return jnp.where(col_ids[None, :] < leading, own, inner)

    blocks = lax.map(
        finish_single,
        (
            points_rows,
            noise_rows,
            basis_rows.reshape(count, width, -1),
            lead_rows.reshape(count, width, leading),
            starts,
        ),
    )
    return blocks.reshape(count * width, ncols)


def body(points, noise, basis):
    ratio = lax.axis_size("rows") // lax.axis_size("cols")
    row_pos = lax.axis_index("rows")
    col_pos = lax.axis_index("cols")
    width = noise.shape[1]
    rows_dev = basis.shape[0]
    row_pts = rows_dev // width
    col_pts = row_pts * ratio
    cols_dev = rows_dev * ratio
    row_start = row_pos * rows_dev
    col_start = col_pos * cols_dev
    row_points = lax.dynamic_slice_in_dim(points, row_pos * row_pts, row_pts, 0)
    row_noise = lax.dynamic_slice_in_dim(noise, row_pos * row_pts, row_pts, 0)
    col_points = lax.dynamic_slice_in_dim(points, col_pos * col_pts, col_pts, 0)
    pieces = []
    for step in range(ratio):
        pieces.append(from_root(basis, "rows", col_pos * ratio + step))
    col_basis = jnp.concatenate(pieces, axis=0)
    lead_points = LEAD // width
    row_starts = row_start + width * jnp.arange(row_pts)
    own_ids = row_start + jnp.arange(rows_dev)
    columns = assemble(
        row_points,
        row_noise,
        basis,
        row_starts,
        col_points[:lead_points],
        col_basis[:LEAD],
        col_start,
    )
    top_ids = jnp.arange(LEAD)
    lead_rows = None
    lead_top = None
    for panel_index in range(PANELS):
        low = panel_index * PW
        block = columns[:, low : low + PW]
        if lead_rows is not None:
            block = block - jnp.dot(
                lead_rows, lead_top[low : low + PW].T, precision=lax.Precision.HIGHEST
            )
        upper = from_root(block[:LEAD], "rows", 0)
        diag = jnp.linalg.cholesky(upper[low : low + PW])
        top_panel = lax.linalg.triangular_solve(
            diag, upper, left_side=False, lower=True, transpose_a=True
        )
        own_panel = lax.linalg.triangular_solve(
            diag, block, left_side=False, lower=True, transpose_a=True
        )
        top_panel = mask_panel(top_panel, top_ids, low)
        own_panel = mask_panel(own_panel, own_ids, low)
        if lead_rows is None:
            lead_rows, lead_top = (own_panel, top_panel)
        else:
            lead_rows = jnp.concatenate([lead_rows, own_panel], axis=1)
            lead_top = jnp.concatenate([lead_top, top_panel], axis=1)
    lead_rows = from_root(lead_rows, "cols", 0)
    copies = []
    for step in range(ratio):
        copies.append(from_root(lead_rows, "rows", col_pos * ratio + step))
    lead_cols = jnp.concatenate(copies, axis=0)
    return finish(
        row_points,
        row_noise,
        basis,
        row_starts,
        lead_rows,
        col_points,
        col_basis,
        col_start,
        lead_cols,
    )


def solution(mesh):
    placed = (P(), P(), P("rows", None))
    return jax.shard_map(
        body, mesh=mesh, in_specs=placed, out_specs=P("rows", "cols"), check_vma=False
    )
```

profile of v0, /device:TPU:16, one launch (start us, length us, event | category | flops | bytes accessed | tf_op | source)
XLA Modules:
  0.0 818.8 jit_solution(1879432131793466496)
XLA Ops:
  9.7 88.5 %all-reduce.13.cloned.1.call-done = f32[1280,128]{1,0:T(8,128)} async-done(((f32[1280,128]{1,0:T(8,128)}), f32[1280,128]{1,0:T(8,128)}) %all-reduce.13.cloned.1.call-update) | async-done | bytes 655376 | tf_op jit(solution)/shard_map/psum | solution.py:13
  99.2 40.4 %while.29 = (s32[]{:T(128)}, f32[10,128,512]{2,1,0:T(8,128)}, f32[10,127]{1,0:T(8,128)S(1)}, f32[4,127]{1,0:T(4,128)S(1)}, f32[10,128,128]{2,1,0:T(8,128)}, /*in...) while((s32[]{:T(128)}, f32[10,128,512]{2,1,0:T(8,128)}, ...), condition=%wide.region_3.4_spmd, body=%wide.region_1.0_spmd.sunk | while | flops 101157744 | bytes 1808469 | solution.py:46
  144.7 81.7 %all-reduce.15.cloned.1.call-done = f32[512,256]{0,1:T(8,128)} async-done(((f32[512,256]{0,1:T(8,128)}), f32[512,256]{0,1:T(8,128)}) %all-reduce.15.cloned.1.call-update) | async-done | bytes 524304 | tf_op jit(solution)/shard_map/psum | solution.py:13
  228.7 11.7 %cholesky.130 = f32[128,128]{1,0:T(8,128)S(1)} custom-call(f32[128,128]{1,0:T(8,128)S(1)} %cholesky.194), custom_call_target="Cholesky" | custom-call | tf_op jit(solution)/shard_map/jit(cholesky)/cholesky | solution.py:136
  240.4 9.8 %custom-call.17 = f32[1,128,128]{1,2,0:T(8,128)S(1)} custom-call(f32[1,128,128]{2,1,0:T(8,128)S(1)} %get-tuple-element.375), custom_call_target="InvertDiagBlocksLowerTriangular" | custom-call | tf_op jit(solution)/shard_map/jit(cholesky)/cholesky | solution.py:136
  250.7 11.7 %cholesky.147 = f32[128,128]{1,0:T(8,128)S(1)} custom-call(f32[128,128]{1,0:T(8,128)S(1)} %convolution_subtract_fusion.6), custom_call_target="Cholesky" | custom-call | tf_op jit(solution)/shard_map/jit(cholesky)/cholesky | solution.py:136
  265.3 5.7 while.31
  271.0 21.1 %custom-call.18 = f32[2,128,128]{1,2,0:T(8,128)} custom-call(f32[2,128,128]{2,1,0:T(8,128)} %get-tuple-element.280), custom_call_target="InvertDiagBlocksLowerTriangular" | custom-call | tf_op jit(solution)/shard_map/triangular_solve/custom-call.0 | solution.py:140
  300.8 84.5 %all-reduce.17.cloned.1.call-done = f32[512,256]{0,1:T(8,128)} async-done(((f32[512,256]{0,1:T(8,128)}), f32[512,256]{0,1:T(8,128)}) %all-reduce.17.cloned.1.call-update) | async-done | bytes 524304 | tf_op jit(solution)/shard_map/psum | solution.py:13
  387.4 11.7 %cholesky.164 = f32[128,128]{1,0:T(8,128)S(1)} custom-call(f32[128,128]{1,0:T(8,128)S(1)} %cholesky.197), custom_call_target="Cholesky" | custom-call | tf_op jit(solution)/shard_map/jit(cholesky)/cholesky | solution.py:136
  399.1 9.8 %custom-call.19 = f32[1,128,128]{1,2,0:T(8,128)S(1)} custom-call(f32[1,128,128]{2,1,0:T(8,128)S(1)} %get-tuple-element.371), custom_call_target="InvertDiagBlocksLowerTriangular" | custom-call | tf_op jit(solution)/shard_map/jit(cholesky)/cholesky | solution.py:136
  409.4 11.7 %cholesky.181 = f32[128,128]{1,0:T(8,128)S(1)} custom-call(f32[128,128]{1,0:T(8,128)S(1)} %convolution_subtract_fusion.5), custom_call_target="Cholesky" | custom-call | tf_op jit(solution)/shard_map/jit(cholesky)/cholesky | solution.py:136
  423.9 4.2 while.32
  428.1 19.7 %custom-call.20 = f32[2,128,128]{1,2,0:T(8,128)S(1)} custom-call(f32[2,128,128]{2,1,0:T(8,128)S(1)} %get-tuple-element.281), custom_call_target="InvertDiagBlocksLowerTriangular" | custom-call | tf_op jit(solution)/shard_map/triangular_solve/custom-call.0 | solution.py:140
  451.9 62.5 %all-reduce.19.cloned.1.call-done = f32[1280,512]{0,1:T(8,128)} async-done(((f32[1280,512]{0,1:T(8,128)}), f32[1280,512]{0,1:T(8,128)}) %all-reduce.19.cloned.1.call-update) | async-done | bytes 2621456 | tf_op jit(solution)/shard_map/psum | solution.py:13
  514.4 4.4 broadcast_select_fusion.1
  522.6 119.4 %all-reduce.21.cloned.1.call-done = (f32[1280,512]{0,1:T(8,128)}, f32[1280,512]{0,1:T(8,128)}, f32[1280,128]{1,0:T(8,128)}) async-done(((f32[1280,512]{0,1:T(8,128)}, f32[1280,512]{0,1:T(8,128)}, f32[1280,128]{1,0:T(8,128)}), (f32[1280,512]{0,1:T(8,128)}, f32[1280,512]{0,1:T(8,128)}, f32[1280,128]{1,0:T(8,128)})) %all-reduce.21.cloned.1.call-update) | async-done | bytes 5898256 | tf_op jit(solution)/shard_map/psum | solution.py:13
  642.0 5.5 maximum_bitcast_fusion
  648.8 162.4 %while.30 = (s32[]{:T(128)}, f32[10,128,2560]{2,1,0:T(8,128)}, f32[10,128,512]{2,1,0:T(8,128)}, s32[10]{0:T(128)S(1)}, f32[512,2560]{1,0:T(8,128)}, /*index=5*/f...) while((s32[]{:T(128)}, f32[10,128,2560]{2,1,0:T(8,128)}, ...), condition=%wide.region_16.19_spmd.clone.clone, body=%wide.region_14.18_spmd.clone.clone.sunk | while | flops 2519910400 | bytes 23683260 | solution.py:82
  658.1 6.9 fusion.100
  674.3 6.9 fusion.100
  685.1 3.2 fusion.99
  690.6 6.9 fusion.100
  701.3 3.2 fusion.99
  706.9 6.9 fusion.100
  717.5 3.2 fusion.99
  723.1 6.9 fusion.100
  739.3 6.9 fusion.100
  755.5 6.9 fusion.100
  771.8 6.9 fusion.100
  788.0 6.9 fusion.100
  804.2 6.9 fusion.100
  (458 shorter events, 161.0 us)
Async XLA Ops:
  6.5 2.4 copy-start
  6.5 91.7 %all-reduce.13.cloned.1.call-start = ((), (), s32[]{:S(2)}) async-start(), calls=%async_computation | async-start | bytes 1310720 | tf_op jit(solution)/shard_map/psum | solution.py:13
  8.8 217.6 %all-reduce.15.cloned.1.call-start = ((), (), s32[]{:S(2)}) async-start(), calls=%async_computation.1 | async-start | bytes 1048576 | tf_op jit(solution)/shard_map/psum | solution.py:13
  141.7 243.5 %all-reduce.17.cloned.1.call-start = ((), (), s32[]{:S(2)}) async-start(), calls=%async_computation.2 | async-start | bytes 1048576 | tf_op jit(solution)/shard_map/psum | solution.py:13
  227.5 64.6 %copy-start.4 = (f32[10,128,512]{2,1,0:T(8,128)S(1)}, f32[10,128,512]{2,1,0:T(8,128)}, u32[]{:S(2)}) copy-start(f32[10,128,512]{2,1,0:T(8,128)} %get-tuple-element.203) | copy-start | bytes 7864324
  262.5 2.0 copy-start.7
  264.5 29.3 %copy-start.5 = (f32[512,256]{0,1:T(8,128)S(1)}, f32[512,256]{0,1:T(8,128)}, u32[]{:S(2)}) copy-start(f32[512,256]{0,1:T(8,128)} %all-reduce.15.cloned.1.call-done) | copy-start | bytes 1572868
  292.1 1.7 copy-start.9
  296.9 1.3 copy-start.3
  300.5 213.9 %all-reduce.19.cloned.1.call-start = ((), (), s32[]{:S(2)}) async-start(), calls=%async_computation.3 | async-start | bytes 5242880 | tf_op jit(solution)/shard_map/psum | solution.py:13
  451.8 190.2 %all-reduce.21.cloned.1.call-start = ((), (), s32[]{:S(2)}) async-start(), calls=%async_computation.4 | async-start | bytes 11796480 | tf_op jit(solution)/shard_map/psum | solution.py:13
  518.8 1.7 copy-start.2
  642.0 5.5 copy-start.6
  642.0 5.5 copy-start.8
  811.1 0.9 copy-start.1
Sparse Core Ops, SparseCore 0:
  10.6 87.5 all-reduce.12
  141.8 84.5 all-reduce.14
  300.7 84.5 all-reduce.16
  451.9 62.4 all-reduce.18
  518.9 123.0 all-reduce.20
where the time goes:
time: 831 us; the launch traced here: 819 us
  waiting for transfers between devices  437 us (53%)
  other arithmetic  152 us (18%)
  matrix products  130 us (16%)
  local copies, waits for them, and re-layouts  74.6 us (9%)
  between operations  16.3 us (2%)
  loops' own time  8.95 us (1%)
    psum x5, waiting for transfers between devices, from_root(): return lax.psum(jnp.where(mine, x, jnp.zeros_like(x)), axis)  437 us
    dot_general x10, matrix products, finish_single(): trail = values - jnp.dot(lrow, cross, precision=lax.Precision.HIGHEST)  69.2 us
    another operation x13, other arithmetic, body(): diag = jnp.linalg.cholesky(upper[low:low + PW])  68.7 us
    dot_general x20, matrix products, point_rows(): jnp.dot(basis_row, col_basis.T, precision=lax.Precision.HIGHEST)  51.1 us
    another operation x5, other arithmetic, body(): lax.linalg.triangular_solve(diag, block, left_side=False, lower=True, tra...  40.8 us
  transfers between devices with their start and end apart: 5, of which 5 were waited for; matrix products, arithmetic and copies ran while one was open for 1% of the time, Pallas kernels for 0%

commit v1 on v0

v1 whole, which is shorter than its diff:
```python
import jax
import jax.numpy as jnp
from jax import lax
from jax.experimental import pallas as pl
from jax.experimental.pallas import tpu as pltpu
from jax.sharding import PartitionSpec as P

W = 128
LEAD = 512
NL = LEAD // W
NR = 10
NC = 20
RG = 16
PIECE = LEAD // RG
MESH = pl.DeviceIdType.MESH
HI = lax.Precision.HIGHEST
F32 = jnp.float32
BF = jnp.bfloat16


def dot(a, b):
    return lax.dot_general(a, b, (((1,), (0,)), ((), ())), precision=HI, preferred_element_type=F32)


def dot_nt(a, b):
    return lax.dot_general(a, b, (((1,), (1,)), ((), ())), precision=HI, preferred_element_type=F32)


def dot_tn(a, b):
    return lax.dot_general(a, b, (((0,), (0,)), ((), ())), precision=HI, preferred_element_type=F32)


def split(x):
    high = x.astype(BF)
    return high, (x - high.astype(F32)).astype(BF)


def spread_kernel(basis_ref, lead_ref, send_a, send_b, recv, local):
    r = lax.axis_index("rows")
    c = lax.axis_index("cols")
    barrier = pltpu.get_barrier_semaphore()
    for off in range(1, RG):
        pl.semaphore_signal(barrier, inc=1, device_id=(lax.rem(r + off, RG), c), device_id_type=MESH)
    pl.semaphore_wait(barrier, RG - 1)

    def first(t):
        rows = pl.ds(PIECE * t, PIECE)
        return pltpu.make_async_remote_copy(
            src_ref=basis_ref.at[rows], dst_ref=lead_ref.at[rows], send_sem=send_a.at[t], recv_sem=recv.at[t],
            device_id=(t, c), device_id_type=MESH)

    def zero(t):
        rows = pl.ds(0, PIECE)
        return pltpu.make_async_remote_copy(
            src_ref=basis_ref.at[rows], dst_ref=lead_ref.at[rows], send_sem=send_b.at[t], recv_sem=recv.at[0],
            device_id=(t, c), device_id_type=MESH)

    def second(off):
        rows = pl.ds(pl.multiple_of(PIECE * r, PIECE), PIECE)
        return pltpu.make_async_remote_copy(
            src_ref=lead_ref.at[rows], dst_ref=lead_ref.at[rows], send_sem=send_b.at[off], recv_sem=recv.at[r],
            device_id=(lax.rem(r + off, RG), c), device_id_type=MESH)

    @pl.when(r == 0)
    def _():
        for t in range(1, RG):
            first(t).start()
        for t in range(1, RG):
            zero(t).start()
        own = pltpu.make_async_copy(basis_ref.at[pl.ds(0, LEAD)], lead_ref, local)
        own.start()
        own.wait()
        for t in range(1, RG):
            first(t).wait_send()
            zero(t).wait_send()

    @pl.when(r != 0)
    def _():
        rows = pl.ds(pl.multiple_of(PIECE * r, PIECE), PIECE)
        pltpu.make_async_remote_copy(
            src_ref=lead_ref.at[rows], dst_ref=lead_ref.at[rows], send_sem=send_a.at[0], recv_sem=recv.at[r],
            device_id=(0, c), device_id_type=MESH).wait_recv()
        for off in range(1, RG):
            @pl.when(r + off != RG)
            def _():
                second(off).start()
        for off in range(1, RG):
            q = lax.rem(r + off, RG)
            rows_q = pl.ds(pl.multiple_of(PIECE * q, PIECE), PIECE)
            pltpu.make_async_remote_copy(
                src_ref=lead_ref.at[rows_q], dst_ref=lead_ref.at[rows_q], send_sem=send_a.at[0], recv_sem=recv.at[q],
                device_id=(0, c), device_id_type=MESH).wait_recv()
        for off in range(1, RG):
            @pl.when(r + off != RG)
            def _():
                second(off).wait_send()


def spread(basis):
    return pl.pallas_call(
        spread_kernel,
        out_shape=jax.ShapeDtypeStruct((LEAD, W), F32),
        in_specs=[pl.BlockSpec(memory_space=pl.ANY)],
        out_specs=pl.BlockSpec(memory_space=pltpu.VMEM),
        scratch_shapes=[
            pltpu.SemaphoreType.DMA((RG,)),
            pltpu.SemaphoreType.DMA((RG,)),
            pltpu.SemaphoreType.DMA((RG,)),
            pltpu.SemaphoreType.DMA,
        ],
        compiler_params=pltpu.CompilerParams(collective_id=0, has_side_effects=True),
    )(basis)


def eye_masks():
    row = lax.broadcasted_iota(jnp.int32, (W, W), 0)
    col = lax.broadcasted_iota(jnp.int32, (W, W), 1)
    same = row == col
    return same, same & (col > 0)


def unit_row():
    return (lax.broadcasted_iota(jnp.int32, (1, W), 1) == 0).astype(F32)


def unit_col():
    return (lax.broadcasted_iota(jnp.int32, (W, 1), 0) == 0).astype(F32)


def kval(a_row, b_row):
    rho = a_row - b_row
    return jnp.exp(-0.5 * jnp.sum(rho * rho, axis=1, keepdims=True))


def tile(k, a_row, b_row, a_col, b_col, jmask):
    p = k * (unit_col() + b_col - a_col)
    q = unit_row() + a_row - b_row
    return jnp.where(jmask, k, 0.0) + p * q


def lane_splat(v, j):
    return jnp.broadcast_to(v[:, j:j + 1], (8, W))


def row_splat(v, j):
    return jnp.broadcast_to(v[j:j + 1, :], (8, W))


def invert_block(read, write):
    n = W // 8
    lane = lax.broadcasted_iota(jnp.int32, (8, W), 1)
    sub = lax.broadcasted_iota(jnp.int32, (8, W), 0)
    rows = {}

    def take(r):
        return rows.pop(r) if r in rows else read(r)

    for k in range(n):
        own = (lane >= 8 * k) & (lane < 8 * k + 8)
        top = take(k)
        cols = [lane_splat(top, 8 * k + j) for j in range(8)]
        if k + 1 < n:
            following = take(k + 1)
            ahead = [lane_splat(following, 8 * k + j) for j in range(8)]
        q = jnp.where(own, (lane - 8 * k == sub).astype(F32), top)
        w = None
        for j in range(8):
            d = row_splat(cols[j], j)
            inv = 1.0 / d
            row_j = row_splat(q, j)
            w_j = row_j * lax.rsqrt(d)
            w = w_j if w is None else jnp.where(sub == j, w_j, w)
            m = jnp.where(sub == j, 1.0 - inv, cols[j] * inv)
            for j2 in range(j + 1, 8):
                cols[j2] = cols[j2] - m * row_splat(cols[j2], j)
            q = q - m * row_j
        write(k, jnp.where(lane <= 8 * k + sub, w, 0.0))
        if k + 1 < n:
            qs = [row_splat(q, j) for j in range(8)]

            def update(v, c):
                t0 = c[0] * qs[0] + c[1] * qs[1]
                t1 = c[2] * qs[2] + c[3] * qs[3]
                t2 = c[4] * qs[4] + c[5] * qs[5]
                t3 = c[6] * qs[6] + c[7] * qs[7]
                return jnp.where(own, 0.0, v) - ((t0 + t1) + (t2 + t3))

            rows[k + 1] = update(following, ahead)
            for r in range(k + 2, n):
                v = take(r)
                rows[r] = update(v, [lane_splat(v, 8 * k + j) for j in range(8)])


def lead_kernel(points_ref, noise_ref, lead_ref, m_ref, g_ref, work, square):
    same, jmask = eye_masks()
    square[...] = jnp.zeros((W, W), F32)
    square[0:8, :] = points_ref[0:8, :]
    turned = square[...].T
    work[...] = dot_nt(lead_ref[...], lead_ref[...])
    for i in range(NL):
        for j in range(NL):
            a_row, b_row = points_ref[i:i + 1, :], points_ref[j:j + 1, :]
            t = tile(kval(a_row, b_row), a_row, b_row, turned[:, i:i + 1], turned[:, j:j + 1], jmask)
            if i == j:
                t = t + jnp.where(same, noise_ref[i:i + 1, :], 0.0)
            work[W * i:W * i + W, W * j:W * j + W] += t
    for p in range(NL):
        lo, hi = W * p, W * p + W

        def write(k, v):
            m_ref[lo + 8 * k:lo + 8 * k + 8, lo:hi] = v

        invert_block(lambda k: work[lo + 8 * k:lo + 8 * k + 8, lo:hi], write)
        inv = m_ref[lo:hi, lo:hi]
        if p:
            m_ref[lo:hi, 0:lo] = dot(inv, work[lo:hi, 0:lo])
        if hi < LEAD:
            m_ref[lo:hi, hi:] = jnp.zeros((W, LEAD - hi), F32)
            u = dot(inv, work[lo:hi, hi:])
            work[hi:, hi:] -= dot_tn(u, u)
            e = dot_tn(u, m_ref[lo:hi, 0:hi])
            if p:
                work[hi:, 0:lo] -= e[:, 0:lo]
            work[hi:, lo:hi] = -e[:, lo:hi]
    g_ref[...] = dot_tn(m_ref[...], m_ref[...])


def lead_inverse(points, noise, lead):
    return pl.pallas_call(
        lead_kernel,
        out_shape=(jax.ShapeDtypeStruct((LEAD, LEAD), F32), jax.ShapeDtypeStruct((LEAD, LEAD), F32)),
        scratch_shapes=[pltpu.VMEM((LEAD, LEAD), F32), pltpu.VMEM((W, W), F32)],
        compiler_params=pltpu.CompilerParams(vmem_limit_bytes=40 << 20),
        cost_estimate=pl.CostEstimate(flops=4 * 10 ** 10, bytes_accessed=4 * 10 ** 6, transcendentals=512),
    )(points, noise, lead)


ROWS_AT, COLS_AT = 8, 32


def finish_kernel(pos, points_ref, noise_ref, basis_ref, lead_ref, m_ref, g_ref, cols0_ref, cols1_ref, out_ref,
                  square, turned, own, h, lhs, panel, kp, coef, kij, rhs):
    r, c, x = pos()
    step = pl.program_id(0)
    same, jmask = eye_masks()
    lane = lax.broadcasted_iota(jnp.int32, (W, W), 1)
    row_idx = lax.broadcasted_iota(jnp.int32, (W, W), 0)

    @pl.when(step == 0)
    def _():
        square[...] = jnp.zeros((W, W), F32)
        square[0:8, :] = points_ref[0:8, :]
        square[ROWS_AT:ROWS_AT + 16, :] = points_ref[pl.ds(NR * r, 16), :]
        square[COLS_AT:COLS_AT + 24, :] = points_ref[pl.ds(NC * c, 24), :]
        t = square[...].T
        turned[...] = t
        colp = square[COLS_AT:COLS_AT + 24, :]
        coef[...] = jnp.zeros((W, LEAD), F32)
        for m in range(NL):
            km = kval(colp, square[m:m + 1, :])
            kij[24 * m:24 * m + 24, :] = jnp.broadcast_to(km, (24, W))
            q = -km * (unit_row() + colp - square[m:m + 1, :])
            coef[0:NC, W * m:W * m + W] = q[0:NC, :]
            coef[NC + NC * m:2 * NC + NC * m, W * m:W * m + W] = q[0:NC, :]
        own[...] = dot_nt(basis_ref[...], lead_ref[...])
        tc = pltpu.roll(t, W - COLS_AT, 1)
        for i in range(NR):
            a_row = square[ROWS_AT + i:ROWS_AT + i + 1, :]
            a_col = t[:, ROWS_AT + i:ROWS_AT + i + 1]
            rows = slice(W * i, W * i + W)
            for l in range(NL):
                b_row = square[l:l + 1, :]
                v = tile(kval(a_row, b_row), a_row, b_row, a_col, t[:, l:l + 1], jmask)
                if i < NL and l == i:
                    v = v + jnp.where(same & (r == 0), noise_ref[l:l + 1, :], 0.0)
                own[rows, W * l:W * l + W] += v
            rho = tc - a_col
            kk = jnp.exp(-0.5 * jnp.sum(rho * rho, axis=0, keepdims=True))
            kij[96 + i:97 + i, :] = kk
            kp[rows, :] = jnp.where(lane < NC, kk * (unit_col() + rho), 0.0)
        for s in range(5):
            rows = slice(256 * s, 256 * s + 256)
            a = own[rows, :]
            hs = dot(a, g_ref[...])
            h[rows, :] = hs
            e = dot_nt(hs, coef[...]) + kp[rows, :]
            b = basis_ref[rows, :] - dot(hs, lead_ref[...])
            eh, el = split(e)
            bh, bl = split(b)
            lhs[rows, 0:128] = bh
            lhs[rows, 128:256] = bh
            lhs[rows, 256:384] = bl
            lhs[rows, 384:512] = eh
            lhs[rows, 512:640] = eh
            lhs[rows, 640:768] = el

        @pl.when(c == 0)
        def _():
            for s in range(5):
                rows = slice(256 * s, 256 * s + 256)
                v = dot_nt(own[rows, :], m_ref[...])
                rid = 256 * s + lax.broadcasted_iota(jnp.int32, (256, LEAD), 0)
                cid = lax.broadcasted_iota(jnp.int32, (256, LEAD), 1)
                panel[rows, :] = jnp.where((r == 0) & (rid < cid), 0.0, v)

    is_panel = (c == 0) & (step < 2)

    @pl.when(is_panel)
    def _():
        out_ref[...] = panel[:, pl.ds(pl.multiple_of(256 * jnp.minimum(step, 1), 256), 256)]

    @pl.when(jnp.logical_not(is_panel))
    def _():
        local = pl.ds(pl.multiple_of(256 * lax.rem(step, 5), 256), 256)
        flip = (x + step // 5) % 2 == 1
        b = jnp.where(flip, cols1_ref[local, :], cols0_ref[local, :])
        bh, bl = split(b)
        rhs[:, 0:128] = bh
        rhs[:, 128:256] = bl
        rhs[:, 256:384] = bh
        for s in range(2):
            j = 2 * step + s
            rows = slice(W * s, W * s + W)
            y = square[pl.ds(COLS_AT + j, 1), :]
            ycol = jnp.sum(jnp.where(same, y, 0.0), axis=1, keepdims=True)
            v = jnp.where(lane == j, unit_col() - ycol, 0.0)
            for m in range(NL):
                v = v + jnp.where(lane == NC + NC * m + j, turned[:, m:m + 1], 0.0)
            vh, vl = split(v)
            rhs[rows, 384:512] = vh
            rhs[rows, 512:640] = vl
            rhs[rows, 640:768] = vh

        def rows_pair(s, carry):
            base = pl.multiple_of(256 * s, 256)
            acc = lax.dot_general(lhs[pl.ds(base, 256), :], rhs[...], (((1,), (1,)), ((), ())), preferred_element_type=F32)
            for ii in range(2):
                i = 2 * s + ii
                at = pl.ds(pl.multiple_of(base + W * ii, W), W)
                y_i = square[pl.ds(ROWS_AT + i, 1), :]
                hi_m = [h[at, W * m:W * m + W] for m in range(NL)]
                kpi = kp[at, :]
                for jj in range(2):
                    j = 2 * step + jj
                    kcol = jnp.sum(jnp.where(lane == j, kpi, 0.0), axis=1, keepdims=True)
                    kk = jnp.sum(jnp.where(lane[0:1] == j, kij[pl.ds(96 + i, 1), :], 0.0), axis=1, keepdims=True)
                    v = acc[W * ii:W * ii + W, W * jj:W * jj + W] + kcol * y_i
                    comb = kij[pl.ds(j, 1), :] * hi_m[0]
                    for m in range(1, NL):
                        comb = comb + kij[pl.ds(24 * m + j, 1), :] * hi_m[m]
                    v = v - jnp.where(lane > 0, comb, 0.0) + jnp.where(jmask, kk, 0.0)
                    out_ref[at, W * jj:W * jj + W] = v

                    @pl.when(NR * r + i == NC * c + j)
                    def _():
                        out_ref[at, W * jj:W * jj + W] += jnp.where(same, noise_ref[pl.ds(NR * r + i, 1), :], 0.0)
            return carry

        lax.fori_loop(0, 5, rows_pair, 0)

        @pl.when(r == 0)
        def _():
            cross = dot_nt(lead_ref[...], b)
            for s in range(2):
                j = 2 * step + s
                b_row = square[pl.ds(COLS_AT + j, 1), :]
                b_col = jnp.sum(jnp.where(same, b_row, 0.0), axis=1, keepdims=True)
                for l in range(NL):
                    a_row = square[l:l + 1, :]
                    v = tile(kval(a_row, b_row), a_row, b_row, turned[:, l:l + 1], b_col, jmask)
                    own[W * l:W * l + W, W * s:W * s + W] = cross[W * l:W * l + W, W * s:W * s + W] + v
            out_ref[0:LEAD, :] = dot(m_ref[...], own[0:LEAD, 0:256])


def finish_call(pos, points, noise, basis, lead, m, g, cols0, cols1):
    rows = NR * W
    full = pl.BlockSpec(memory_space=pltpu.VMEM)
    return pl.pallas_call(
        lambda *refs: finish_kernel(pos, *refs),
        grid=(NC // 2,),
        out_shape=jax.ShapeDtypeStruct((rows, NC * W), F32),
        in_specs=[full] * 8,
        out_specs=pl.BlockSpec((rows, 2 * W), lambda s: (0, s)),
        scratch_shapes=[
            pltpu.VMEM((W, W), F32),
            pltpu.VMEM((W, W), F32),
            pltpu.VMEM((rows, LEAD), F32),
            pltpu.VMEM((rows, LEAD), F32),
            pltpu.VMEM((rows, 6 * W), BF),
            pltpu.VMEM((rows, LEAD), F32),
            pltpu.VMEM((rows, W), F32),
            pltpu.VMEM((W, LEAD), F32),
            pltpu.VMEM((112, W), F32),
            pltpu.VMEM((2 * W, 6 * W), BF),
        ],
        compiler_params=pltpu.CompilerParams(vmem_limit_bytes=52 << 20),
    )(points, noise, basis, lead, m, g, cols0, cols1)


def permute_pairs(t):
    pairs = []
    for z in range(4):
        for x in range(4):
            for y in range(4):
                for k in range(2):
                    source = (4 * y + 2 * k + (t + x) % 2) * 8 + ((2 * y + 2 - z) % 4) * 2 + x // 2
                    pairs.append((source, (4 * z + x) * 8 + 2 * y + k))
    return pairs


def body(points, noise, basis):
    points = jnp.pad(points, ((0, 32), (1, 0)))
    cols0 = lax.ppermute(basis, ("rows", "cols"), permute_pairs(0))
    cols1 = lax.ppermute(basis, ("rows", "cols"), permute_pairs(1))
    lead = spread(basis)
    m, g = lead_inverse(points, noise, lead)

    def pos():
        r = lax.axis_index("rows")
        return r, lax.axis_index("cols"), lax.rem(r, 4)

    return finish_call(pos, points, noise, basis, lead, m, g, cols0, cols1)


def solution(mesh):
    placed = (P(), P(), P("rows", None))
    return jax.shard_map(body, mesh=mesh, in_specs=placed, out_specs=P("rows", "cols"), check_vma=False)
```

time: 831 us -> 162 us (0.19)
  the two profiles are of different devices: /device:TPU:16 before, /device:TPU:0 now
where the time goes in v1:
time: 162 us; the launch traced here: 161 us
  Pallas kernels  148 us (91%)
  starting transfers between devices  8.08 us (5%)
  local copies, waits for them, and re-layouts  5.65 us (3%)
    pallas_call x1, Pallas kernels, finish_call(): pl.pallas_call(lambda *refs: finish_kernel(pos, *refs), grid=(NC // 2,),...  65.4 us
    pallas_call x1, Pallas kernels, spread(): pl.pallas_call(spread_kernel, out_shape=jax.ShapeDtypeStruct((LEAD, W), F...  57 us
    pallas_call x1, Pallas kernels, lead_inverse(): pl.pallas_call(lead_kernel, out_shape=(jax.ShapeDtypeStruct((LEAD, LEAD),...  25.1 us
    unnamed x16, local copies, waits for them, and re-layouts  4.68 us
    ppermute x1, starting transfers between devices, body(): cols1 = lax.ppermute(basis, ('rows', 'cols'), permute_pairs(1))  4.12 us
    ppermute x1, starting transfers between devices, body(): cols0 = lax.ppermute(basis, ('rows', 'cols'), permute_pairs(0))  3.96 us
  transfers between devices with their start and end apart: 2, of which 0 were waited for; matrix products, arithmetic and copies ran while one was open for 1% of the time, Pallas kernels for 51%

profile of v1, /device:TPU:0, one launch (start us, length us, event | category | flops | bytes accessed | tf_op | source)
XLA Modules:
  0.0 161.3 jit_solution(3493667411678319442)
XLA Ops:
  0.0 4.0 %collective-permute-start = (f32[1280,128]{1,0:T(8,128)}, f32[1280,128]{1,0:T(8,128)S(1)}, u32[]{:S(2)}, u32[]{:S(2)}) collective-permute-start(f32[1280,128]{1,0:T(8,128)} %refs_2_.1), channel_id=1, source_target_pairs={{4,0},{20,1},{32,2},{48,3},{68,4},{84,5},{96,6},{112,7},{12,8},{28... | collective-permute-start | bytes 1966088 | tf_op jit(solution)/shard_map/ppermute | solution.py:413
  4.0 4.1 %collective-permute-start.1 = (f32[1280,128]{1,0:T(8,128)}, f32[1280,128]{1,0:T(8,128)S(1)}, u32[]{:S(2)}, u32[]{:S(2)}) collective-permute-start(f32[1280,128]{1,0:T(8,128)} %refs_2_.1), channel_id=1, source_target_pairs={{12,0},{28,1},{40,2},{56,3},{76,4},{92,5},{104,6},{120,7},{4,8},{2... | collective-permute-start | bytes 1966088 | tf_op jit(solution)/shard_map/ppermute | solution.py:414
  8.1 57.0 %shard_map.37.lead_ref.refs_3_ = f32[512,128]{1,0:T(8,128)} custom-call(f32[1280,128]{1,0:T(8,128)} %refs_2_.1), custom_call_target="tpu_custom_call" | custom-call | tf_op jit(solution)/shard_map/pallas_call | solution.py:100
  65.1 1.0 pad.4.points_ref.refs_0_
  66.1 0.0 copy-start.1
  66.1 0.9 copy-done.1
  67.0 0.0 copy-start.5
  67.0 0.9 copy-done.5
  67.9 0.0 copy-start
  67.9 0.0 copy-start.2
  67.9 0.0 copy-start.6
  67.9 25.1 %shard_map.38 = (f32[512,512]{1,0:T(8,128)S(1)}, f32[512,512]{1,0:T(8,128)S(1)}) custom-call(f32[192,128]{1,0:T(8,128)S(1)} %pad.4.points_ref.refs_0_, f32[160,128]{1,0:T(8,128)S(1)} %copy-done.5, f32[512,128]{1,0:T(8,128)S(1)} %copy-done.1), custom_call_target="tpu_custom_call" | custom-call | flops 40000000000 | bytes 4000000 | tf_op jit(solution)/shard_map/pallas_call | solution.py:229
  93.1 0.0 copy-start.3
  93.1 1.0 copy-done.3
  94.0 0.0 copy-start.4
  94.0 1.0 copy-done.4
  95.0 0.0 collective-permute-done.refs_6_
  95.1 0.0 collective-permute-done.1.refs_7_
  95.1 0.0 copy-start.7
  95.1 0.8 copy-done.7
  95.9 0.0 copy-done
  95.9 0.0 copy-done.2
  95.9 0.0 copy-done.6
  95.9 65.4 %shard_map.39 = f32[1280,2560]{1,0:T(8,128)} custom-call(f32[192,128]{1,0:T(8,128)S(1)} %pad.4.points_ref.refs_0_, f32[160,128]{1,0:T(8,128)S(1)} %copy-done.6, f32[1280,128]{1,0:T(8,128)S(1)} %copy-done, f32[512,128]{1,0:T(8,128)S(1)} %copy-done.2, f32[512,512]{1,0:T(8,128)} %copy-done.3, f32[512,512]{1,0:T(8,128)} %copy-done.4, ...), custom_call_target="tpu_custom_call" | custom-call | tf_op jit(solution)/shard_map/pallas_call | solution.py:378
Async XLA Ops:
  0.0 95.1 %collective-permute-start = (f32[1280,128]{1,0:T(8,128)}, f32[1280,128]{1,0:T(8,128)S(1)}, u32[]{:S(2)}, u32[]{:S(2)}) collective-permute-start(f32[1280,128]{1,0:T(8,128)} %refs_2_.1), channel_id=1, source_target_pairs={{4,0},{20,1},{32,2},{48,3},{68,4},{84,5},{96,6},{112,7},{12,8},{28... | collective-permute-start | bytes 1966088 | tf_op jit(solution)/shard_map/ppermute | solution.py:413
  4.0 91.1 %collective-permute-start.1 = (f32[1280,128]{1,0:T(8,128)}, f32[1280,128]{1,0:T(8,128)S(1)}, u32[]{:S(2)}, u32[]{:S(2)}) collective-permute-start(f32[1280,128]{1,0:T(8,128)} %refs_2_.1), channel_id=1, source_target_pairs={{12,0},{28,1},{40,2},{56,3},{76,4},{92,5},{104,6},{120,7},{4,8},{2... | collective-permute-start | bytes 1966088 | tf_op jit(solution)/shard_map/ppermute | solution.py:414
  66.1 1.0 copy-start.1
  67.0 0.9 copy-start.5
  67.9 28.0 %copy-start = (f32[1280,128]{1,0:T(8,128)S(1)}, f32[1280,128]{1,0:T(8,128)}, u32[]{:S(2)}) copy-start(f32[1280,128]{1,0:T(8,128)} %refs_2_.1) | copy-start | bytes 1966084
  67.9 28.0 %copy-start.2 = (f32[512,128]{1,0:T(8,128)S(1)}, f32[512,128]{1,0:T(8,128)}, u32[]{:S(2)}) copy-start(f32[512,128]{1,0:T(8,128)} %shard_map.37.lead_ref.refs_3_) | copy-start | bytes 786436
  67.9 28.0 %copy-start.6 = (f32[160,128]{1,0:T(8,128)S(1)}, f32[160,128]{1,0:T(8,128)}, u32[]{:S(2)}) copy-start(f32[160,128]{1,0:T(8,128)} %refs_1_.1) | copy-start | bytes 245764
  93.1 1.0 copy-start.3
  94.0 1.0 copy-start.4
  95.1 0.9 copy-start.7

commit v2 on v1

v2 whole, which is shorter than its diff:
```python
import jax
import jax.numpy as jnp
from jax import lax
from jax.experimental import pallas as pl
from jax.experimental.pallas import tpu as pltpu
from jax.sharding import PartitionSpec as P

W = 128
LEAD = 512
NL = LEAD // W
NR = 10
NC = 20
RG = 16
HALF = LEAD // 2
PIECE = HALF // RG
BLOCK_HALF = NR * W // 2
CHUNKS = 4
CHUNK = BLOCK_HALF // CHUNKS
MESH = pl.DeviceIdType.MESH
HI = lax.Precision.HIGHEST
F32 = jnp.float32
BF = jnp.bfloat16


def dot(a, b):
    return lax.dot_general(a, b, (((1,), (0,)), ((), ())), precision=HI, preferred_element_type=F32)


def dot_nt(a, b):
    return lax.dot_general(a, b, (((1,), (1,)), ((), ())), precision=HI, preferred_element_type=F32)


def dot_tn(a, b):
    return lax.dot_general(a, b, (((0,), (0,)), ((), ())), precision=HI, preferred_element_type=F32)


def split(x):
    high = x.astype(BF)
    return high, (x - high.astype(F32)).astype(BF)


class Moves:
    def __init__(self, basis, lead, stage, cols, sems):
        self.basis, self.lead, self.stage, self.cols = basis, lead, stage, cols
        (self.first_sem, self.second_sem, self.lead_recv, self.half_sem, self.local_sem,
         self.a_send, self.a_recv, self.b_send, self.b_recv) = sems
        self.r = lax.axis_index("rows")
        self.c = lax.axis_index("cols")
        self.z, self.x = self.r // 4, self.r % 4
        self.y, self.k = self.c // 2, self.c % 2
        self.home = self.x // 2

    def barrier(self):
        sem = pltpu.get_barrier_semaphore()
        for off in range(1, RG):
            pl.semaphore_signal(sem, inc=1, device_id=((self.r + off) % RG, self.c), device_id_type=MESH)
        for x in range(4):
            pl.semaphore_signal(sem, inc=1, device_id=(4 * self.z + x, 2 * self.y + 1 - self.k), device_id_type=MESH)
        pl.semaphore_wait(sem, RG + 3)

    def piece(self, source, q, send_sem, target):
        rows = pl.ds(pl.multiple_of(HALF * self.k + PIECE * q, PIECE), PIECE)
        return pltpu.make_async_remote_copy(
            src_ref=source.at[rows], dst_ref=self.lead.at[rows], send_sem=send_sem, recv_sem=self.lead_recv.at[q],
            device_id=(target, self.c), device_id_type=MESH)

    def exchange(self, core):
        rows = pl.ds(pl.multiple_of(HALF * core, HALF), HALF)
        return pltpu.make_async_remote_copy(
            src_ref=self.lead.at[rows], dst_ref=self.lead.at[rows], send_sem=self.half_sem.at[0], recv_sem=self.half_sem.at[1],
            device_id=(self.r, 2 * self.y + 1 - self.k), device_id_type=MESH)

    def spread_lead(self):
        r = self.r

        @pl.when(r == 0)
        def _():
            for t in range(1, RG):
                self.piece(self.basis, t, self.first_sem.at[t], t).start()
            for t in range(1, RG):
                self.piece(self.basis, 0, self.second_sem.at[t], t).start()
            own = pltpu.make_async_copy(self.basis.at[pl.ds(0, LEAD)], self.lead, self.local_sem.at[0])
            own.start()
            own.wait()
            for t in range(1, RG):
                self.piece(self.basis, t, self.first_sem.at[t], t).wait_send()
                self.piece(self.basis, 0, self.second_sem.at[t], t).wait_send()

        @pl.when(r != 0)
        def _():
            self.piece(self.lead, r, self.first_sem.at[0], 0).wait_recv()
            for off in range(1, RG):
                @pl.when(r + off != RG)
                def _():
                    self.piece(self.lead, r, self.second_sem.at[off], (r + off) % RG).start()
            for off in range(1, RG):
                self.piece(self.lead, (r + off) % RG, self.first_sem.at[0], 0).wait_recv()
            self.exchange(self.k).start()
            self.exchange(1 - self.k).wait_recv()
            self.exchange(self.k).wait_send()
            for off in range(1, RG):
                @pl.when(r + off != RG)
                def _():
                    self.piece(self.lead, r, self.second_sem.at[off], (r + off) % RG).wait_send()

    def own_rows(self, n):
        return pl.ds(pl.multiple_of(BLOCK_HALF * self.k + CHUNK * n, CHUNK), CHUNK)

    def along_z(self, n, dz):
        return pltpu.make_async_remote_copy(
            src_ref=self.basis.at[self.own_rows(n)], dst_ref=self.stage.at[pl.ds(CHUNK * n, CHUNK)],
            send_sem=self.a_send.at[n, dz], recv_sem=self.a_recv.at[n],
            device_id=(4 * ((self.z + dz) % 4) + self.x, self.c), device_id_type=MESH)

    def keep(self, n):
        return pltpu.make_async_copy(self.basis.at[self.own_rows(n)], self.stage.at[pl.ds(CHUNK * n, CHUNK)], self.local_sem.at[1 + n])

    def start_z(self):
        @pl.when(self.z == self.y)
        def _():
            for n in range(CHUNKS):
                for dz in (1, 3, 2):
                    self.along_z(n, dz).start()
                self.keep(n).start()

    def place(self, block, half, n):
        return pl.ds(pl.multiple_of(2 * BLOCK_HALF * block + BLOCK_HALF * half + CHUNK * n, CHUNK), CHUNK)

    def along_x(self, n, dx):
        return pltpu.make_async_remote_copy(
            src_ref=self.stage.at[pl.ds(CHUNK * n, CHUNK)], dst_ref=self.cols.at[self.place(self.x % 2, self.k, n)],
            send_sem=self.b_send.at[n, dx], recv_sem=self.b_recv.at[self.x % 2, self.k, n],
            device_id=(4 * self.z + (self.x + dx) % 4, 2 * self.y + self.home), device_id_type=MESH)

    def settle(self, n):
        return pltpu.make_async_copy(self.stage.at[pl.ds(CHUNK * n, CHUNK)], self.cols.at[self.place(self.x % 2, self.k, n)], self.local_sem.at[1 + CHUNKS + n])

    def forward(self, n):
        @pl.when(self.z == self.y)
        def _():
            self.keep(n).wait()

        @pl.when(self.z != self.y)
        def _():
            self.along_z(n, 1).wait_recv()

        for dx in (1, 3, 2):
            self.along_x(n, dx).start()

        @pl.when(self.home == self.k)
        def _():
            self.settle(n).start()

        @pl.when(self.home != self.k)
        def _():
            self.along_x(n, 0).start()

    def finish(self):
        for n in range(CHUNKS):
            for block in range(2):
                for half in range(2):
                    mine = (self.home == self.k) & (self.x % 2 == block) & (self.k == half)

                    @pl.when(jnp.logical_not(mine))
                    def _():
                        rows = self.place(block, half, n)
                        pltpu.make_async_remote_copy(
                            src_ref=self.cols.at[rows], dst_ref=self.cols.at[rows], send_sem=self.b_send.at[n, 0],
                            recv_sem=self.b_recv.at[block, half, n],
                            device_id=(self.r, 2 * self.y + 1 - self.k), device_id_type=MESH).wait_recv()
        for n in range(CHUNKS):
            for dx in (1, 3, 2):
                self.along_x(n, dx).wait_send()

            @pl.when(self.home == self.k)
            def _():
                self.settle(n).wait()

            @pl.when(self.home != self.k)
            def _():
                self.along_x(n, 0).wait_send()

            @pl.when(self.z == self.y)
            def _():
                for dz in (1, 3, 2):
                    self.along_z(n, dz).wait_send()


def eye_masks():
    row = lax.broadcasted_iota(jnp.int32, (W, W), 0)
    col = lax.broadcasted_iota(jnp.int32, (W, W), 1)
    same = row == col
    return same, same & (col > 0)


def unit_row():
    return (lax.broadcasted_iota(jnp.int32, (1, W), 1) == 0).astype(F32)


def unit_col():
    return (lax.broadcasted_iota(jnp.int32, (W, 1), 0) == 0).astype(F32)


def kval(a_row, b_row):
    rho = a_row - b_row
    return jnp.exp(-0.5 * jnp.sum(rho * rho, axis=1, keepdims=True))


def tile(k, a_row, b_row, a_col, b_col, jmask):
    p = k * (unit_col() + b_col - a_col)
    q = unit_row() + a_row - b_row
    return jnp.where(jmask, k, 0.0) + p * q


def lane_splat(v, j):
    return jnp.broadcast_to(v[:, j:j + 1], (8, W))


def row_splat(v, j):
    return jnp.broadcast_to(v[j:j + 1, :], (8, W))


def invert_block(read, write):
    n = W // 8
    lane = lax.broadcasted_iota(jnp.int32, (8, W), 1)
    sub = lax.broadcasted_iota(jnp.int32, (8, W), 0)
    rows = {}

    def take(r):
        return rows.pop(r) if r in rows else read(r)

    for k in range(n):
        own = (lane >= 8 * k) & (lane < 8 * k + 8)
        top = take(k)
        cols = [lane_splat(top, 8 * k + j) for j in range(8)]
        if k + 1 < n:
            following = take(k + 1)
            ahead = [lane_splat(following, 8 * k + j) for j in range(8)]
        q = jnp.where(own, (lane - 8 * k == sub).astype(F32), top)
        w = None
        for j in range(8):
            d = row_splat(cols[j], j)
            inv = 1.0 / d
            row_j = row_splat(q, j)
            w_j = row_j * lax.rsqrt(d)
            w = w_j if w is None else jnp.where(sub == j, w_j, w)
            m = jnp.where(sub == j, 1.0 - inv, cols[j] * inv)
            for j2 in range(j + 1, 8):
                cols[j2] = cols[j2] - m * row_splat(cols[j2], j)
            q = q - m * row_j
        write(k, jnp.where(lane <= 8 * k + sub, w, 0.0))
        if k + 1 < n:
            qs = [row_splat(q, j) for j in range(8)]

            def update(v, c):
                t0 = c[0] * qs[0] + c[1] * qs[1]
                t1 = c[2] * qs[2] + c[3] * qs[3]
                t2 = c[4] * qs[4] + c[5] * qs[5]
                t3 = c[6] * qs[6] + c[7] * qs[7]
                return jnp.where(own, 0.0, v) - ((t0 + t1) + (t2 + t3))

            rows[k + 1] = update(following, ahead)
            for r in range(k + 2, n):
                v = take(r)
                rows[r] = update(v, [lane_splat(v, 8 * k + j) for j in range(8)])


def lead_kernel(points_ref, noise_ref, basis_ref, lead_ref, cols_ref, m_ref, g_ref, work, square, stage, *sems):
    moves = Moves(basis_ref, lead_ref, stage, cols_ref, sems)
    moves.barrier()
    moves.spread_lead()
    moves.start_z()

    def after(p):
        if p < 2:
            for n in range(CHUNKS // 2):
                moves.forward(CHUNKS // 2 * p + n)

    factor(points_ref, noise_ref, lead_ref, m_ref, g_ref, work, square, after)
    moves.finish()


def factor(points_ref, noise_ref, lead_ref, m_ref, g_ref, work, square, after):
    same, jmask = eye_masks()
    square[...] = jnp.zeros((W, W), F32)
    square[0:8, :] = points_ref[0:8, :]
    turned = square[...].T
    work[...] = dot_nt(lead_ref[...], lead_ref[...])
    for i in range(NL):
        for j in range(NL):
            a_row, b_row = points_ref[i:i + 1, :], points_ref[j:j + 1, :]
            t = tile(kval(a_row, b_row), a_row, b_row, turned[:, i:i + 1], turned[:, j:j + 1], jmask)
            if i == j:
                t = t + jnp.where(same, noise_ref[i:i + 1, :], 0.0)
            work[W * i:W * i + W, W * j:W * j + W] += t
    for p in range(NL):
        lo, hi = W * p, W * p + W

        def write(k, v):
            m_ref[lo + 8 * k:lo + 8 * k + 8, lo:hi] = v

        invert_block(lambda k: work[lo + 8 * k:lo + 8 * k + 8, lo:hi], write)
        inv = m_ref[lo:hi, lo:hi]
        if p:
            m_ref[lo:hi, 0:lo] = dot(inv, work[lo:hi, 0:lo])
        if hi < LEAD:
            m_ref[lo:hi, hi:] = jnp.zeros((W, LEAD - hi), F32)
            u = dot(inv, work[lo:hi, hi:])
            work[hi:, hi:] -= dot_tn(u, u)
            e = dot_tn(u, m_ref[lo:hi, 0:hi])
            if p:
                work[hi:, 0:lo] -= e[:, 0:lo]
            work[hi:, lo:hi] = -e[:, lo:hi]
        after(p)
    g_ref[...] = dot_tn(m_ref[...], m_ref[...])


def lead_inverse(points, noise, basis):
    vmem = pl.BlockSpec(memory_space=pltpu.VMEM)
    dma = pltpu.SemaphoreType.DMA
    return pl.pallas_call(
        lead_kernel,
        out_shape=(
            jax.ShapeDtypeStruct((LEAD, W), F32),
            jax.ShapeDtypeStruct((NC * W, W), F32),
            jax.ShapeDtypeStruct((LEAD, LEAD), F32),
            jax.ShapeDtypeStruct((LEAD, LEAD), F32),
        ),
        in_specs=[vmem, vmem, pl.BlockSpec(memory_space=pl.ANY)],
        out_specs=(vmem,) * 4,
        scratch_shapes=[
            pltpu.VMEM((LEAD, LEAD), F32),
            pltpu.VMEM((W, W), F32),
            pltpu.VMEM((BLOCK_HALF, W), F32),
            dma((RG,)),
            dma((RG,)),
            dma((RG,)),
            dma((2,)),
            dma((1 + 2 * CHUNKS,)),
            dma((CHUNKS, 4)),
            dma((CHUNKS,)),
            dma((CHUNKS, 4)),
            dma((2, 2, CHUNKS)),
        ],
        compiler_params=pltpu.CompilerParams(collective_id=0, has_side_effects=True, vmem_limit_bytes=24 << 20),
        cost_estimate=pl.CostEstimate(flops=4 * 10 ** 10, bytes_accessed=4 * 10 ** 6, transcendentals=512),
    )(points, noise, basis)


def factor_only(points, noise, lead):
    return pl.pallas_call(
        lambda p, n, l, m, g, work, square: factor(p, n, l, m, g, work, square, lambda q: None),
        out_shape=(jax.ShapeDtypeStruct((LEAD, LEAD), F32), jax.ShapeDtypeStruct((LEAD, LEAD), F32)),
        scratch_shapes=[pltpu.VMEM((LEAD, LEAD), F32), pltpu.VMEM((W, W), F32)],
        compiler_params=pltpu.CompilerParams(vmem_limit_bytes=24 << 20),
    )(points, noise, lead)


ROWS_AT, COLS_AT = 8, 32
NT = NL + NR


def three_left(x):
    high, low = split(x)
    return jnp.concatenate([high, high, low], axis=1)


def three_right(x, axis):
    high, low = split(x)
    return jnp.concatenate([high, low, high], axis=axis)


def bdot(a, b):
    return lax.dot_general(a, b, (((1,), (0,)), ((), ())), preferred_element_type=F32)


def bdot_nt(a, b):
    return lax.dot_general(a, b, (((1,), (1,)), ((), ())), preferred_element_type=F32)


def finish_kernel(pos, points_ref, noise_ref, basis_ref, lead_ref, m_ref, g_ref, cols_ref, out_ref,
                  square, turned, own, h, lhs, panel, kp, table, rhs, g3, f3, m3):
    r, c = pos()
    step = pl.program_id(0)
    same, jmask = eye_masks()
    lane = lax.broadcasted_iota(jnp.int32, (W, W), 1)

    @pl.when(step == 0)
    def _():
        square[...] = jnp.zeros((W, W), F32)
        square[0:8, :] = points_ref[0:8, :]
        square[ROWS_AT:ROWS_AT + 16, :] = points_ref[pl.ds(NR * r, 16), :]
        square[COLS_AT:COLS_AT + 24, :] = points_ref[pl.ds(NC * c, 24), :]
        t = square[...].T
        turned[...] = t
        colp = square[COLS_AT:COLS_AT + 24, :]
        coef = []
        total = []
        for m in range(NL):
            km = kval(colp, square[m:m + 1, :])
            table[m, :, :] = jnp.broadcast_to(km, (24, W))
            q = (-km * (unit_row() + colp - square[m:m + 1, :]))[0:24]
            total.append(q)
            pieces = [q if n == m else jnp.zeros((24, W), F32) for n in range(NL)]
            coef.append(jnp.concatenate(pieces, axis=1))
        weights = jnp.concatenate([jnp.concatenate(total, axis=1)] + coef + [jnp.zeros((W - 24 * (NL + 1), LEAD), F32)], axis=0)
        f3[0:W, :] = three_right(weights, 1)
        f3[W:2 * W, :] = three_right(lead_ref[...].T, 1)
        g3[...] = three_right(g_ref[...], 0)
        b3 = three_left(basis_ref[...])
        l3 = three_right(lead_ref[...], 1)
        own[...] = bdot_nt(b3, l3)
        tc = pltpu.roll(t, W - COLS_AT, 1)
        for i in range(NR):
            a_row = square[ROWS_AT + i:ROWS_AT + i + 1, :]
            a_col = t[:, ROWS_AT + i:ROWS_AT + i + 1]
            rows = slice(W * i, W * i + W)
            for l in range(NL):
                b_row = square[l:l + 1, :]
                v = tile(kval(a_row, b_row), a_row, b_row, a_col, t[:, l:l + 1], jmask)
                if l == i:
                    v = v + jnp.where(same & (r == 0), noise_ref[l:l + 1, :], 0.0)
                own[rows, W * l:W * l + W] += v
            rho = tc - a_col
            kk = jnp.exp(-0.5 * jnp.sum(rho * rho, axis=0, keepdims=True))
            kp[rows, :] = jnp.where(lane < NC, kk * (unit_col() + rho), 0.0)
            table[NL + i, :, :] = jnp.broadcast_to(kval(colp, a_row), (24, W))
            h[rows, LEAD:LEAD + W] = jnp.where(jmask, -1.0, 0.0) + a_col * a_row
        for s in range(5):
            rows = slice(256 * s, 256 * s + 256)
            hs = bdot(three_left(own[rows, :]), g3[...])
            for m in range(NL):
                h[rows, W * m:W * m + W] = jnp.where(lax.broadcasted_iota(jnp.int32, (256, W), 1) > 0, hs[:, W * m:W * m + W], 0.0)
            eb = bdot_nt(three_left(hs), f3[...])
            lhs[rows, 0:3 * W] = three_left(basis_ref[rows, :] - eb[:, W:])
            lhs[rows, 3 * W:] = three_left(eb[:, 0:W] + kp[rows, :])

        @pl.when((c == 0) | (r == 0))
        def _():
            m3[...] = three_left(m_ref[...])

        @pl.when(c == 0)
        def _():
            for s in range(5):
                rows = slice(256 * s, 256 * s + 256)
                v = bdot_nt(three_right(own[rows, :], 1), m3[...])
                rid = 256 * s + lax.broadcasted_iota(jnp.int32, (256, LEAD), 0)
                cid = lax.broadcasted_iota(jnp.int32, (256, LEAD), 1)
                panel[rows, :] = jnp.where((r == 0) & (rid < cid), 0.0, v)

    is_panel = (c == 0) & (step < 2)

    @pl.when(is_panel)
    def _():
        out_ref[...] = panel[:, pl.ds(pl.multiple_of(256 * jnp.minimum(step, 1), 256), 256)]

    @pl.when(jnp.logical_not(is_panel))
    def _():
        b = cols_ref[pl.ds(pl.multiple_of(256 * step, 256), 256), :]
        rhs[:, 0:3 * W] = three_right(b, 1)
        bases = []
        for s in range(2):
            j = 2 * step + s
            y = square[pl.ds(COLS_AT + j, 1), :]
            ycol = jnp.sum(jnp.where(same, y, 0.0), axis=1, keepdims=True)
            bases.append(jnp.broadcast_to(unit_col() + ycol, (W, W)))
            v = jnp.where(lane == j, unit_col() - ycol, 0.0)
            for m in range(NL):
                v = v + jnp.where(lane == 24 + 24 * m + j, turned[:, m:m + 1], 0.0)
            rhs[W * s:W * s + W, 3 * W:] = three_right(v, 1)

        def rows_block(s):
            rows = slice(256 * s, 256 * s + 256)
            acc = bdot_nt(lhs[rows, :], rhs[...])
            for ii in range(2):
                i = 2 * s + ii
                at = slice(W * i, W * i + W)
                y_i = square[ROWS_AT + i:ROWS_AT + i + 1, :]
                his = [h[at, W * m:W * m + W] for m in range(NL + 1)]
                for jj in range(2):
                    ks = [table[m, pl.ds(2 * step + jj, 1), :] for m in range(NL)]
                    ks.append(table[NL + i, pl.ds(2 * step + jj, 1), :])
                    v = acc[W * ii:W * ii + W, W * jj:W * jj + W] + bases[jj] * (ks[NL] * y_i)
                    comb = (ks[0] * his[0] + ks[1] * his[1]) + (ks[2] * his[2] + ks[3] * his[3])
                    out_ref[at, W * jj:W * jj + W] = v - (comb + ks[4] * his[4])

        @pl.when(r == 0)
        def _():
            cross = bdot_nt(three_left(lead_ref[...]), rhs[:, 0:3 * W])
            for s in range(2):
                b_row = square[pl.ds(COLS_AT + 2 * step + s, 1), :]
                b_col = bases[s][:, 0:1] - unit_col()
                for l in range(NL):
                    a_row = square[l:l + 1, :]
                    v = tile(kval(a_row, b_row), a_row, b_row, turned[:, l:l + 1], b_col, jmask)
                    own[W * l:W * l + W, W * s:W * s + W] = cross[W * l:W * l + W, W * s:W * s + W] + v
            out_ref[0:LEAD, :] = bdot(m3[...], three_right(own[0:LEAD, 0:256], 0))
            for s in range(2, 5):
                rows_block(s)

        @pl.when(r != 0)
        def _():
            for s in range(5):
                rows_block(s)

        for s in range(2):
            i = NC * c + 2 * step + s - NR * r

            @pl.when((i >= 0) & (i < NR) & ((r > 0) | (i >= NL)))
            def _():
                at = pl.ds(pl.multiple_of(W * i, W), W)
                out_ref[at, W * s:W * s + W] += jnp.where(same, noise_ref[pl.ds(NR * r + i, 1), :], 0.0)


def finish_call(pos, points, noise, basis, lead, m, g, cols):
    rows = NR * W
    full = pl.BlockSpec(memory_space=pltpu.VMEM)
    return pl.pallas_call(
        lambda *refs: finish_kernel(pos, *refs),
        grid=(NC // 2,),
        out_shape=jax.ShapeDtypeStruct((rows, NC * W), F32),
        in_specs=[full] * 7,
        out_specs=pl.BlockSpec((rows, 2 * W), lambda s: (0, s)),
        scratch_shapes=[
            pltpu.VMEM((W, W), F32),
            pltpu.VMEM((W, W), F32),
            pltpu.VMEM((rows, LEAD), F32),
            pltpu.VMEM((rows, LEAD + W), F32),
            pltpu.VMEM((rows, 6 * W), BF),
            pltpu.VMEM((rows, LEAD), F32),
            pltpu.VMEM((rows, W), F32),
            pltpu.VMEM((NT, 24, W), F32),
            pltpu.VMEM((2 * W, 6 * W), BF),
            pltpu.VMEM((3 * LEAD, LEAD), BF),
            pltpu.VMEM((2 * W, 3 * LEAD), BF),
            pltpu.VMEM((LEAD, 3 * LEAD), BF),
        ],
        compiler_params=pltpu.CompilerParams(vmem_limit_bytes=40 << 20),
    )(points, noise, basis, lead, m, g, cols)


def body(points, noise, basis):
    points = jnp.pad(points, ((0, 32), (1, 0)))
    lead, cols, m, g = lead_inverse(points, noise, basis)

    def pos():
        return lax.axis_index("rows"), lax.axis_index("cols")

    return finish_call(pos, points, noise, basis, lead, m, g, cols)


def solution(mesh):
    placed = (P(), P(), P("rows", None))
    return jax.shard_map(body, mesh=mesh, in_specs=placed, out_specs=P("rows", "cols"), check_vma=False)
```

time: 162 us -> 76.2 us (0.47)
  the two profiles are of different devices: /device:TPU:0 before, /device:TPU:16 now
where the time goes in v2:
time: 76.2 us; the launch traced here: 76 us
  Pallas kernels  73 us (96%)
  local copies, waits for them, and re-layouts  2.95 us (4%)
    pallas_call x1, Pallas kernels, lead_inverse(): pl.pallas_call(lead_kernel, out_shape=(jax.ShapeDtypeStruct((LEAD, W), F3...  47.8 us
    pallas_call x1, Pallas kernels, finish_call(): pl.pallas_call(lambda *refs: finish_kernel(pos, *refs), grid=(NC // 2,),...  25.2 us
    unnamed x8, local copies, waits for them, and re-layouts  1.98 us

profile of v2, /device:TPU:16, one launch (start us, length us, event | category | flops | bytes accessed | tf_op | source)
XLA Modules:
  0.0 76.0 jit_solution(7181718957752247373)
XLA Ops:
  0.0 1.0 %pad.4.points_ref.refs_0_ = f32[192,128]{1,0:T(8,128)S(1)} pad(f32[160,127]{1,0:T(8,128)} %param.3, f32[]{:T(128)} %constant.2.clone.1), padding=0_32x1_0 | pad | bytes 179588 | tf_op jit(solution)/shard_map/jit(_pad)/pad | solution.py:543
  1.0 0.0 copy-start
  1.0 1.1 %copy-done = f32[1280,128]{1,0:T(8,128)S(1)} copy-done((f32[1280,128]{1,0:T(8,128)S(1)}, f32[1280,128]{1,0:T(8,128)}, u32[]{:S(2)}) %copy-start) | copy-done | bytes 655384
  2.1 0.0 copy-start.2
  2.1 0.9 %copy-done.2 = f32[160,128]{1,0:T(8,128)S(1)} copy-done((f32[160,128]{1,0:T(8,128)S(1)}, f32[160,128]{1,0:T(8,128)}, u32[]{:S(2)}) %copy-start.2) | copy-done | bytes 81944
  3.0 0.0 copy-start.1
  3.0 0.0 copy-start.3
  3.0 47.8 %shard_map.37 = (f32[512,128]{1,0:T(8,128)S(1)}, f32[2560,128]{1,0:T(8,128)S(1)}, f32[512,512]{1,0:T(8,128)S(1)}, f32[512,512]{1,0:T(8,128)S(1)}) custom-call(f32[192,128]{1,0:T(8,128)S(1)} %pad.4.points_ref.refs_0_, f32[160,128]{1,0:T(8,128)S(1)} %copy-done.2, f32[1280,128]{1,0:T(8,128)S(1)} %copy-done), custom_call_target="tpu_custom_call" | custom-call | flops 40000000000 | bytes 4000000 | tf_op jit(solution)/shard_map/pallas_call | solution.py:321
  50.8 0.0 copy-done.1
  50.8 0.0 copy-done.3
  50.8 25.2 %shard_map.38 = f32[1280,2560]{1,0:T(8,128)} custom-call(f32[192,128]{1,0:T(8,128)S(1)} %pad.4.points_ref.refs_0_, f32[160,128]{1,0:T(8,128)S(1)} %copy-done.3, f32[1280,128]{1,0:T(8,128)S(1)} %copy-done.1, f32[512,128]{1,0:T(8,128)S(1)} %get-tuple-element.9.refs_3_, f32[512,512]{1,0:T(8,128)S(1)} %get-tuple-element.10.refs_4_, ...), custom_call_target="tpu_custom_call" | custom-call | tf_op jit(solution)/shard_map/pallas_call | solution.py:518
Async XLA Ops:
  1.0 1.1 %copy-start = (f32[1280,128]{1,0:T(8,128)S(1)}, f32[1280,128]{1,0:T(8,128)}, u32[]{:S(2)}) copy-start(f32[1280,128]{1,0:T(8,128)} %refs_2_.1) | copy-start | bytes 1966084
  2.1 0.9 %copy-start.2 = (f32[160,128]{1,0:T(8,128)S(1)}, f32[160,128]{1,0:T(8,128)}, u32[]{:S(2)}) copy-start(f32[160,128]{1,0:T(8,128)} %refs_1_.1) | copy-start | bytes 245764
  3.0 47.8 %copy-start.1 = (f32[1280,128]{1,0:T(8,128)S(1)}, f32[1280,128]{1,0:T(8,128)}, u32[]{:S(2)}) copy-start(f32[1280,128]{1,0:T(8,128)} %refs_2_.1) | copy-start | bytes 1966084
  3.0 47.8 %copy-start.3 = (f32[160,128]{1,0:T(8,128)S(1)}, f32[160,128]{1,0:T(8,128)}, u32[]{:S(2)}) copy-start(f32[160,128]{1,0:T(8,128)} %refs_1_.1) | copy-start | bytes 245764

commit v3 on v2

v3 whole, which is shorter than its diff:
```python
from types import SimpleNamespace

import jax
import jax.numpy as jnp
from jax import lax
from jax.experimental import pallas as pl
from jax.experimental.pallas import tpu as pltpu
from jax.sharding import PartitionSpec as P

W = 128
LEAD = 512
NL = LEAD // W
NR = 10
NC = 20
RG = 16
HALF = LEAD // 2
PIECE = HALF // RG
BLOCK_HALF = NR * W // 2
CHUNKS = 4
CHUNK = BLOCK_HALF // CHUNKS
MESH = pl.DeviceIdType.MESH
HI = lax.Precision.HIGHEST
F32 = jnp.float32
BF = jnp.bfloat16


def dot(a, b):
    return lax.dot_general(a, b, (((1,), (0,)), ((), ())), precision=HI, preferred_element_type=F32)


def dot_nt(a, b):
    return lax.dot_general(a, b, (((1,), (1,)), ((), ())), precision=HI, preferred_element_type=F32)


def dot_tn(a, b):
    return lax.dot_general(a, b, (((0,), (0,)), ((), ())), precision=HI, preferred_element_type=F32)


def split(x):
    high = x.astype(BF)
    return high, (x - high.astype(F32)).astype(BF)


class Moves:
    def __init__(self, basis, lead, stage, cols, sems):
        self.basis, self.lead, self.stage, self.cols = basis, lead, stage, cols
        (self.first_sem, self.second_sem, self.lead_recv, self.half_sem, self.local_sem,
         self.a_send, self.a_recv, self.b_send, self.b_recv) = sems
        self.r = lax.axis_index("rows")
        self.c = lax.axis_index("cols")
        self.z, self.x = self.r // 4, self.r % 4
        self.y, self.k = self.c // 2, self.c % 2
        self.home = self.x // 2

    def barrier(self):
        sem = pltpu.get_barrier_semaphore()
        for off in range(1, RG):
            pl.semaphore_signal(sem, inc=1, device_id=((self.r + off) % RG, self.c), device_id_type=MESH)
        for x in range(4):
            pl.semaphore_signal(sem, inc=1, device_id=(4 * self.z + x, 2 * self.y + 1 - self.k), device_id_type=MESH)
        pl.semaphore_wait(sem, RG + 3)

    def piece(self, source, q, send_sem, target):
        rows = pl.ds(pl.multiple_of(HALF * self.k + PIECE * q, PIECE), PIECE)
        return pltpu.make_async_remote_copy(
            src_ref=source.at[rows], dst_ref=self.lead.at[rows], send_sem=send_sem, recv_sem=self.lead_recv.at[q],
            device_id=(target, self.c), device_id_type=MESH)

    def exchange(self, core):
        rows = pl.ds(pl.multiple_of(HALF * core, HALF), HALF)
        return pltpu.make_async_remote_copy(
            src_ref=self.lead.at[rows], dst_ref=self.lead.at[rows], send_sem=self.half_sem.at[0], recv_sem=self.half_sem.at[1],
            device_id=(self.r, 2 * self.y + 1 - self.k), device_id_type=MESH)

    def start_spread(self):
        @pl.when(self.r == 0)
        def _():
            for t in range(1, RG):
                self.piece(self.basis, t, self.first_sem.at[t], t).start()
            for t in range(1, RG):
                self.piece(self.basis, 0, self.second_sem.at[t], t).start()
            pltpu.make_async_copy(self.basis.at[pl.ds(0, LEAD)], self.lead, self.local_sem.at[0]).start()

        @pl.when(self.r != 0)
        def _():
            self.piece(self.lead, self.r, self.first_sem.at[0], 0).wait_recv()
            for off in range(1, RG):
                @pl.when(self.r + off != RG)
                def _():
                    self.piece(self.lead, self.r, self.second_sem.at[off], (self.r + off) % RG).start()

    def finish_spread(self):
        @pl.when(self.r == 0)
        def _():
            pltpu.make_async_copy(self.basis.at[pl.ds(0, LEAD)], self.lead, self.local_sem.at[0]).wait()
            for t in range(1, RG):
                self.piece(self.basis, t, self.first_sem.at[t], t).wait_send()
                self.piece(self.basis, 0, self.second_sem.at[t], t).wait_send()

        @pl.when(self.r != 0)
        def _():
            for off in range(1, RG):
                self.piece(self.lead, (self.r + off) % RG, self.first_sem.at[0], 0).wait_recv()
            self.exchange(self.k).start()
            self.exchange(1 - self.k).wait_recv()
            self.exchange(self.k).wait_send()
            for off in range(1, RG):
                @pl.when(self.r + off != RG)
                def _():
                    self.piece(self.lead, self.r, self.second_sem.at[off], (self.r + off) % RG).wait_send()

    def own_rows(self, n):
        return pl.ds(pl.multiple_of(BLOCK_HALF * self.k + CHUNK * n, CHUNK), CHUNK)

    def along_z(self, n, dz):
        return pltpu.make_async_remote_copy(
            src_ref=self.basis.at[self.own_rows(n)], dst_ref=self.stage.at[pl.ds(CHUNK * n, CHUNK)],
            send_sem=self.a_send.at[n, dz], recv_sem=self.a_recv.at[n],
            device_id=(4 * ((self.z + dz) % 4) + self.x, self.c), device_id_type=MESH)

    def keep(self, n):
        return pltpu.make_async_copy(self.basis.at[self.own_rows(n)], self.stage.at[pl.ds(CHUNK * n, CHUNK)], self.local_sem.at[1 + n])

    def start_z(self):
        @pl.when(self.z == self.y)
        def _():
            for n in range(CHUNKS):
                for dz in (1, 3, 2):
                    self.along_z(n, dz).start()
                self.keep(n).start()

    def place(self, block, half, n):
        return pl.ds(pl.multiple_of(2 * BLOCK_HALF * block + BLOCK_HALF * half + CHUNK * n, CHUNK), CHUNK)

    def along_x(self, n, dx):
        return pltpu.make_async_remote_copy(
            src_ref=self.stage.at[pl.ds(CHUNK * n, CHUNK)], dst_ref=self.cols.at[self.place(self.x % 2, self.k, n)],
            send_sem=self.b_send.at[n, dx], recv_sem=self.b_recv.at[self.x % 2, self.k, n],
            device_id=(4 * self.z + (self.x + dx) % 4, 2 * self.y + self.home), device_id_type=MESH)

    def settle(self, n):
        return pltpu.make_async_copy(self.stage.at[pl.ds(CHUNK * n, CHUNK)], self.cols.at[self.place(self.x % 2, self.k, n)], self.local_sem.at[1 + CHUNKS + n])

    def forward(self, n):
        @pl.when(self.z == self.y)
        def _():
            self.keep(n).wait()

        @pl.when(self.z != self.y)
        def _():
            self.along_z(n, 1).wait_recv()

        for dx in (1, 3, 2):
            self.along_x(n, dx).start()

        @pl.when(self.home == self.k)
        def _():
            self.settle(n).start()

        @pl.when(self.home != self.k)
        def _():
            self.along_x(n, 0).start()

    def finish(self):
        for n in range(CHUNKS):
            for block in range(2):
                for half in range(2):
                    mine = (self.home == self.k) & (self.x % 2 == block) & (self.k == half)

                    @pl.when(jnp.logical_not(mine))
                    def _():
                        rows = self.place(block, half, n)
                        pltpu.make_async_remote_copy(
                            src_ref=self.cols.at[rows], dst_ref=self.cols.at[rows], send_sem=self.b_send.at[n, 0],
                            recv_sem=self.b_recv.at[block, half, n],
                            device_id=(self.r, 2 * self.y + 1 - self.k), device_id_type=MESH).wait_recv()
        for n in range(CHUNKS):
            for dx in (1, 3, 2):
                self.along_x(n, dx).wait_send()

            @pl.when(self.home == self.k)
            def _():
                self.settle(n).wait()

            @pl.when(self.home != self.k)
            def _():
                self.along_x(n, 0).wait_send()

            @pl.when(self.z == self.y)
            def _():
                for dz in (1, 3, 2):
                    self.along_z(n, dz).wait_send()


def eye_masks():
    row = lax.broadcasted_iota(jnp.int32, (W, W), 0)
    col = lax.broadcasted_iota(jnp.int32, (W, W), 1)
    same = row == col
    return same, same & (col > 0)


def unit_row():
    return (lax.broadcasted_iota(jnp.int32, (1, W), 1) == 0).astype(F32)


def unit_col():
    return (lax.broadcasted_iota(jnp.int32, (W, 1), 0) == 0).astype(F32)


def kval(a_row, b_row):
    rho = a_row - b_row
    return jnp.exp(-0.5 * jnp.sum(rho * rho, axis=1, keepdims=True))


def tile(k, a_row, b_row, a_col, b_col, jmask):
    p = k * (unit_col() + b_col - a_col)
    q = unit_row() + a_row - b_row
    return jnp.where(jmask, k, 0.0) + p * q


def lane_splat(v, j):
    return jnp.broadcast_to(v[:, j:j + 1], (8, W))


def row_splat(v, j):
    return jnp.broadcast_to(v[j:j + 1, :], (8, W))


def invert_block(read, write):
    n = W // 8
    lane = lax.broadcasted_iota(jnp.int32, (8, W), 1)
    sub = lax.broadcasted_iota(jnp.int32, (8, W), 0)
    rows = {}

    def take(r):
        return rows[r] if r in rows else read(r)

    cols = [lane_splat(take(0), j) for j in range(8)]
    for k in range(n):
        own = (lane >= 8 * k) & (lane < 8 * k + 8)
        last = k + 1 == n
        if not last:
            following = take(k + 1)
            ahead = [lane_splat(following, 8 * k + j) for j in range(8)]
            below = list(ahead)
            later = [lane_splat(following, 8 * k + 8 + j) for j in range(8)]
        q = jnp.where(own, (lane - 8 * k == sub).astype(F32), take(k))
        w = scale = None
        for j in range(8):
            d = row_splat(cols[j], j)
            inv = 1.0 / d
            row_j = row_splat(q, j)
            others = jnp.where(sub == j, 0.0, cols[j])
            pivots = {j2: row_splat(cols[j2], j) for j2 in range(j + 1, 8)}
            for j2 in range(j + 1, 8):
                cols[j2] = cols[j2] - inv * (others * pivots[j2])
            q = q - inv * (others * row_j)
            w_j = row_j * lax.rsqrt(d)
            w = w_j if w is None else jnp.where(sub == j, w_j, w)
            scale = inv if scale is None else jnp.where(sub == j, inv, scale)
            if not last:
                m = below[j] * inv
                for j2 in range(j + 1, 8):
                    below[j2] = below[j2] - m * pivots[j2]
                for j2 in range(8):
                    later[j2] = later[j2] - m * row_splat(below[j], j2)
        write(k, jnp.where(lane <= 8 * k + sub, w, 0.0))
        rows.pop(k, None)
        if not last:
            q = q * scale
            qs = [row_splat(q, j) for j in range(8)]

            def update(v, c):
                t0 = c[0] * qs[0] + c[1] * qs[1]
                t1 = c[2] * qs[2] + c[3] * qs[3]
                t2 = c[4] * qs[4] + c[5] * qs[5]
                t3 = c[6] * qs[6] + c[7] * qs[7]
                return jnp.where(own, 0.0, v) - ((t0 + t1) + (t2 + t3))

            rows[k + 1] = update(following, ahead)
            cols = later
            for r in range(k + 2, n):
                v = take(r)
                rows[r] = update(v, [lane_splat(v, 8 * k + j) for j in range(8)])


ROWS_AT, COLS_AT = 8, 32
NT = NL + NR
ROWS = NR * W


def three_left(x):
    high, low = split(x)
    return jnp.concatenate([high, high, low], axis=1)


def three_right(x, axis):
    high, low = split(x)
    return jnp.concatenate([high, low, high], axis=axis)


def bdot(a, b):
    return lax.dot_general(a, b, (((1,), (0,)), ((), ())), preferred_element_type=F32)


def bdot_nt(a, b):
    return lax.dot_general(a, b, (((1,), (1,)), ((), ())), preferred_element_type=F32)


def prepare_points(r, c, v):
    same, jmask = eye_masks()
    lane = lax.broadcasted_iota(jnp.int32, (W, W), 1)
    square = v.square
    square[...] = jnp.zeros((W, W), F32)
    square[0:8, :] = v.padded[0:8, :]
    square[ROWS_AT:ROWS_AT + 16, :] = v.padded[pl.ds(NR * r, 16), :]
    square[COLS_AT:COLS_AT + 24, :] = v.padded[pl.ds(NC * c, 24), :]
    t = square[...].T
    for i in range(NL):
        for j in range(NL):
            a_row, b_row = square[i:i + 1, :], square[j:j + 1, :]
            part = tile(kval(a_row, b_row), a_row, b_row, t[:, i:i + 1], t[:, j:j + 1], jmask)
            if i == j:
                part = part + jnp.where(same, v.noise[i:i + 1, :], 0.0)
            v.work[W * i:W * i + W, W * j:W * j + W] = part
    colp = square[COLS_AT:COLS_AT + 24, :]
    coef = []
    total = []
    for m in range(NL):
        km = kval(colp, square[m:m + 1, :])
        v.table[m, :, :] = jnp.broadcast_to(km, (24, W))
        q = -km * (unit_row() + colp - square[m:m + 1, :])
        total.append(q)
        pieces = [q if n == m else jnp.zeros((24, W), F32) for n in range(NL)]
        coef.append(jnp.concatenate(pieces, axis=1))
    weights = jnp.concatenate([jnp.concatenate(total, axis=1)] + coef + [jnp.zeros((W - 24 * (NL + 1), LEAD), F32)], axis=0)
    v.f3[0:W, :] = three_right(weights, 1)
    tc = pltpu.roll(t, W - COLS_AT, 1)
    for i in range(NR):
        a_row = square[ROWS_AT + i:ROWS_AT + i + 1, :]
        a_col = t[:, ROWS_AT + i:ROWS_AT + i + 1]
        rows = slice(W * i, W * i + W)
        for l in range(NL):
            b_row = square[l:l + 1, :]
            part = tile(kval(a_row, b_row), a_row, b_row, a_col, t[:, l:l + 1], jmask)
            if l == i:
                part = part + jnp.where(same & (r == 0), v.noise[l:l + 1, :], 0.0)
            v.own[rows, W * l:W * l + W] = part
        rho = tc - a_col
        kk = jnp.exp(-0.5 * jnp.sum(rho * rho, axis=0, keepdims=True))
        v.kp[rows, :] = jnp.where((lane < NC) & ((r > 0) | (i >= NL)), kk * (unit_col() + rho), 0.0)
        alive = jnp.where(r == 0, 0.0, 1.0) if i < NL else 1.0
        v.table[NL + i, :, :] = jnp.broadcast_to(kval(colp, a_row) * alive, (24, W))
        v.h[rows, LEAD:LEAD + W] = jnp.where(jmask, -1.0, 0.0) + a_col * a_row


def factor(v, after):
    work, m_ref = v.work, v.m
    work[...] += dot_nt(v.lead[...], v.lead[...])
    for p in range(NL):
        lo, hi = W * p, W * p + W

        def write(k, x):
            m_ref[lo + 8 * k:lo + 8 * k + 8, lo:hi] = x

        invert_block(lambda k: work[lo + 8 * k:lo + 8 * k + 8, lo:hi], write)
        inv = m_ref[lo:hi, lo:hi]
        if p:
            m_ref[lo:hi, 0:lo] = dot(inv, work[lo:hi, 0:lo])
        if hi < LEAD:
            m_ref[lo:hi, hi:] = jnp.zeros((W, LEAD - hi), F32)
            u = dot(inv, work[lo:hi, hi:])
            work[hi:, hi:] -= dot_tn(u, u)
            e = dot_tn(u, m_ref[lo:hi, 0:hi])
            if p:
                work[hi:, 0:lo] -= e[:, 0:lo]
            work[hi:, lo:hi] = -e[:, lo:hi]
        after(p)


def prepare_rows(r, c, v):
    for s in range(NR // 2):
        rows = slice(2 * W * s, 2 * W * s + 2 * W)
        v.own[rows, :] += bdot_nt(three_left(v.basis[rows, :]), v.l3[...])
    g = bdot(three_left(v.m[...].T), three_right(v.m[...], 0))
    g3 = three_right(g, 0)
    for s in range(NR // 2):
        rows = slice(2 * W * s, 2 * W * s + 2 * W)
        hs = bdot(three_left(v.own[rows, :]), g3)
        b = v.basis[rows, :]
        if s < NL // 2:
            hs = jnp.where(r == 0, -v.m[rows, :], hs)
            b = jnp.where(r == 0, 0.0, b)
        for m in range(NL):
            v.h[rows, W * m:W * m + W] = jnp.where(lax.broadcasted_iota(jnp.int32, (2 * W, W), 1) > 0, hs[:, W * m:W * m + W], 0.0)
        eb = bdot_nt(three_left(hs), v.f3[...])
        v.lhs[rows, 0:3 * W] = three_left(b - eb[:, W:])
        v.lhs[rows, 3 * W:] = three_left(eb[:, 0:W] + v.kp[rows, :])

    @pl.when(c == 0)
    def _():
        m3 = three_left(v.m[...])
        for s in range(NR // 2):
            rows = slice(2 * W * s, 2 * W * s + 2 * W)
            x = bdot_nt(three_right(v.own[rows, :], 1), m3)
            rid = 2 * W * s + lax.broadcasted_iota(jnp.int32, (2 * W, LEAD), 0)
            cid = lax.broadcasted_iota(jnp.int32, (2 * W, LEAD), 1)
            v.panel[rows, :] = jnp.where((r == 0) & (rid < cid), 0.0, x)


def pad_points(v, raw):
    n = raw.shape[0]
    v.padded[0:n, :] = jnp.concatenate([jnp.zeros((n, 1), F32), raw[...]], axis=1)
    v.padded[n:, :] = jnp.zeros((v.padded.shape[0] - n, W), F32)


def lead_products(v):
    v.l3[...] = three_right(v.lead[...], 1)
    v.f3[W:2 * W, :] = three_right(v.lead[...].T, 1)


OUTS = (("square", (W, W), F32), ("table", (NT, 24, W), F32), ("h", (ROWS, LEAD + W), F32), ("lhs", (ROWS, 6 * W), BF),
        ("panel", (ROWS, LEAD), F32))
WORK = (("padded", (192, W), F32), ("lead", (LEAD, W), F32), ("noise", (8, W), F32), ("basis", (ROWS, W), F32),
        ("m", (LEAD, LEAD), F32), ("work", (LEAD, LEAD), F32), ("own", (ROWS, LEAD), F32), ("kp", (ROWS, W), F32),
        ("f3", (2 * W, 3 * LEAD), BF), ("l3", (LEAD, 3 * W), BF))


def lead_kernel(points_hbm, noise_hbm, basis_hbm, *refs):
    n = len(OUTS)
    v = SimpleNamespace(**dict(zip([o[0] for o in OUTS], refs[:n])))
    cols_ref = refs[n]
    refs = refs[n + 1:]
    for spec, ref in zip(WORK, refs):
        setattr(v, spec[0], ref)
    stage, raw, in_sem, *sems = refs[len(WORK):]
    moves = Moves(basis_hbm, v.lead, stage, cols_ref, sems)
    copies = [
        pltpu.make_async_copy(points_hbm, raw, in_sem.at[0]),
        pltpu.make_async_copy(noise_hbm.at[pl.ds(0, 8)], v.noise, in_sem.at[1]),
        pltpu.make_async_copy(basis_hbm, v.basis, in_sem.at[2]),
    ]
    for copy in copies:
        copy.start()
    moves.barrier()
    moves.start_spread()
    for copy in copies:
        copy.wait()
    pad_points(v, raw)
    prepare_points(moves.r, moves.c, v)
    moves.finish_spread()
    moves.start_z()
    lead_products(v)

    def after(p):
        if p < 2:
            for n in range(CHUNKS // 2):
                moves.forward(CHUNKS // 2 * p + n)

    factor(v, after)
    prepare_rows(moves.r, moves.c, v)
    moves.finish()


def prepare(points, noise, basis):
    vmem = pl.BlockSpec(memory_space=pltpu.VMEM)
    dma = pltpu.SemaphoreType.DMA
    return pl.pallas_call(
        lead_kernel,
        out_shape=tuple(jax.ShapeDtypeStruct(o[1], o[2]) for o in OUTS) + (jax.ShapeDtypeStruct((NC * W, W), F32),),
        in_specs=[pl.BlockSpec(memory_space=pl.ANY)] * 3,
        out_specs=(vmem,) * (len(OUTS) + 1),
        scratch_shapes=[pltpu.VMEM(o[1], o[2]) for o in WORK] + [
            pltpu.VMEM((BLOCK_HALF, W), F32),
            pltpu.VMEM(points.shape, F32),
            dma((3,)),
            dma((RG,)),
            dma((RG,)),
            dma((RG,)),
            dma((2,)),
            dma((1 + 2 * CHUNKS,)),
            dma((CHUNKS, 4)),
            dma((CHUNKS,)),
            dma((CHUNKS, 4)),
            dma((2, 2, CHUNKS)),
        ],
        compiler_params=pltpu.CompilerParams(collective_id=0, has_side_effects=True, vmem_limit_bytes=32 << 20),
    )(points, noise, basis)


def finish_kernel(pos, square, table, h, lhs, panel, cols_ref, noise_ref, out_ref, rhs):
    r, c = pos()
    step = pl.program_id(0)
    same, _ = eye_masks()
    is_panel = (c == 0) & (step < 2)

    @pl.when(is_panel)
    def _():
        out_ref[...] = panel[:, pl.ds(pl.multiple_of(256 * jnp.minimum(step, 1), 256), 256)]

    @pl.when(jnp.logical_not(is_panel))
    def _():
        b = cols_ref[pl.ds(pl.multiple_of(256 * step, 256), 256), :]
        rhs[0:3 * W, :] = three_right(b.T, 0)
        bases = []
        row_idx = lax.broadcasted_iota(jnp.int32, (W, W), 0)
        for s in range(2):
            j = 2 * step + s
            y = square[pl.ds(COLS_AT + j, 1), :]
            ycol = jnp.sum(jnp.where(same, y, 0.0), axis=1, keepdims=True)
            bases.append(jnp.broadcast_to(unit_col() + ycol, (W, W)))
            v = jnp.where(row_idx == j, unit_row() - y, 0.0)
            for m in range(NL):
                v = v + jnp.where(row_idx == 24 + 24 * m + j, square[m:m + 1, :], 0.0)
            rhs[3 * W:, W * s:W * s + W] = three_right(v, 0)

        def rows_block(s):
            rows = slice(256 * s, 256 * s + 256)
            acc = bdot(lhs[rows, :], rhs[...])
            for ii in range(2):
                i = 2 * s + ii
                at = slice(W * i, W * i + W)
                y_i = square[ROWS_AT + i:ROWS_AT + i + 1, :]
                his = [h[at, W * m:W * m + W] for m in range(NL + 1)]
                for jj in range(2):
                    ks = [table[m, pl.ds(2 * step + jj, 1), :] for m in range(NL)]
                    ks.append(table[NL + i, pl.ds(2 * step + jj, 1), :])
                    v = acc[W * ii:W * ii + W, W * jj:W * jj + W] + bases[jj] * (ks[NL] * y_i)
                    comb = (ks[0] * his[0] + ks[1] * his[1]) + (ks[2] * his[2] + ks[3] * his[3])
                    out_ref[at, W * jj:W * jj + W] = v - (comb + ks[4] * his[4])

        for s in range(5):
            rows_block(s)

        for s in range(2):
            i = NC * c + 2 * step + s - NR * r

            @pl.when((i >= 0) & (i < NR) & ((r > 0) | (i >= NL)))
            def _():
                at = pl.ds(pl.multiple_of(W * i, W), W)
                out_ref[at, W * s:W * s + W] += jnp.where(same, noise_ref[pl.ds(NR * r + i, 1), :], 0.0)


def finish_call(pos, prepared, noise):
    full = pl.BlockSpec(memory_space=pltpu.VMEM)
    return pl.pallas_call(
        lambda *refs: finish_kernel(pos, *refs),
        grid=(NC // 2,),
        out_shape=jax.ShapeDtypeStruct((ROWS, NC * W), F32),
        in_specs=[full] * 7,
        out_specs=pl.BlockSpec((ROWS, 2 * W), lambda s: (0, s)),
        scratch_shapes=[pltpu.VMEM((6 * W, 2 * W), BF)],
        compiler_params=pltpu.CompilerParams(vmem_limit_bytes=32 << 20),
    )(*prepared, noise)


def body(points, noise, basis):
    prepared = prepare(points, noise, basis)

    def pos():
        return lax.axis_index("rows"), lax.axis_index("cols")

    return finish_call(pos, prepared, noise)


def solution(mesh):
    placed = (P(), P(), P("rows", None))
    return jax.shard_map(body, mesh=mesh, in_specs=placed, out_specs=P("rows", "cols"), check_vma=False)
```

time: 76.2 us -> 65.7 us (0.86)
  Pallas kernels: 73 us -> 61.7 us
  local copies, waits for them, and re-layouts: 2.95 us -> 3.74 us
    pallas_call x1, Pallas kernels: 25.2 us -> 11.7 us  [finish_call(): pl.pallas_call(lambda *refs: finish_kernel(pos, *refs), grid=(NC // 2,),...]
    pallas_call x1, Pallas kernels: 47.8 us -> 50 us  [prepare(): pl.pallas_call(lead_kernel, out_shape=tuple((jax.ShapeDtypeStruct(o[1], o...]
    unnamed x8, local copies, waits for them, and re-layouts: 1.98 us -> 3.74 us
    pad x1 -> x0, local copies, waits for them, and re-layouts: 0.97 us -> none  [body(): points = jnp.pad(points, ((0, 32), (1, 0)))]
where the time goes in v3:
time: 65.7 us; the launch traced here: 65.4 us
  Pallas kernels  61.7 us (94%)
  local copies, waits for them, and re-layouts  3.74 us (6%)
    pallas_call x1, Pallas kernels, prepare(): pl.pallas_call(lead_kernel, out_shape=tuple((jax.ShapeDtypeStruct(o[1], o...  50 us
    pallas_call x1, Pallas kernels, finish_call(): pl.pallas_call(lambda *refs: finish_kernel(pos, *refs), grid=(NC // 2,),...  11.7 us
    unnamed x8, local copies, waits for them, and re-layouts  3.74 us

profile of v3, /device:TPU:16, one launch (start us, length us, event | category | flops | bytes accessed | tf_op | source)
XLA Modules:
  0.0 65.4 jit_solution(15031028121685843960)
XLA Ops:
  0.0 0.0 copy-start
  0.0 1.1 %copy-done = f32[1280,128]{1,0:T(8,128)S(1)} copy-done((f32[1280,128]{1,0:T(8,128)S(1)}, f32[1280,128]{1,0:T(8,128)}, u32[]{:S(2)}) %copy-start) | copy-done | bytes 655384
  1.1 0.0 copy-start.1
  1.1 0.9 %copy-done.1 = f32[160,128]{1,0:T(8,128)S(1)} copy-done((f32[160,128]{1,0:T(8,128)S(1)}, f32[160,128]{1,0:T(8,128)}, u32[]{:S(2)}) %copy-start.1) | copy-done | bytes 81944
  2.0 0.0 copy-start.3
  2.0 0.9 %copy-done.3 = f32[160,127]{1,0:T(8,128)S(1)} copy-done((f32[160,127]{1,0:T(8,128)S(1)}, f32[160,127]{1,0:T(8,128)}, u32[]{:S(2)}) %copy-start.3) | copy-done | bytes 81304
  2.9 50.0 %shard_map.37 = (f32[128,128]{1,0:T(8,128)S(1)}, f32[14,24,128]{2,1,0:T(8,128)S(1)}, f32[1280,640]{1,0:T(8,128)S(1)}, bf16[1280,768]{1,0:T(8,128)(2,1)S(1)}, f32...) custom-call(f32[160,127]{1,0:T(8,128)S(1)} %copy-done.3, f32[160,128]{1,0:T(8,128)S(1)} %copy-done.1, f32[1280,128]{1,0:T(8,128)S(1)} %copy-done), custom_call_target="tpu_custom_call" | custom-call | tf_op jit(solution)/shard_map/pallas_call | solution.py:468
  52.9 0.0 copy-start.2
  52.9 0.9 %copy-done.2 = f32[160,128]{1,0:T(8,128)S(1)} copy-done((f32[160,128]{1,0:T(8,128)S(1)}, f32[160,128]{1,0:T(8,128)}, u32[]{:S(2)}) %copy-start.2) | copy-done | bytes 81944
  53.7 11.7 %shard_map.38 = f32[1280,2560]{1,0:T(8,128)} custom-call(f32[128,128]{1,0:T(8,128)S(1)} %get-tuple-element.11.refs_0_, f32[14,24,128]{2,1,0:T(8,128)S(1)} %get-tuple-element.12.refs_1_, f32[1280,640]{1,0:T(8,128)S(1)} %get-tuple-element.13.refs_2_, bf16[1280,768]{1,0:T(8,128)(2,1)S(1)} %get-tuple-element.14.refs_3_, ...), custom_call_target="tpu_custom_call" | custom-call | tf_op jit(solution)/shard_map/pallas_call | solution.py:546
Async XLA Ops:
  0.0 1.1 %copy-start = (f32[1280,128]{1,0:T(8,128)S(1)}, f32[1280,128]{1,0:T(8,128)}, u32[]{:S(2)}) copy-start(f32[1280,128]{1,0:T(8,128)} %basis_hbm.1) | copy-start | bytes 1966084
  1.1 0.9 %copy-start.1 = (f32[160,128]{1,0:T(8,128)S(1)}, f32[160,128]{1,0:T(8,128)}, u32[]{:S(2)}) copy-start(f32[160,128]{1,0:T(8,128)} %refs_6_.1) | copy-start | bytes 245764
  2.0 0.9 %copy-start.3 = (f32[160,127]{1,0:T(8,128)S(1)}, f32[160,127]{1,0:T(8,128)}, u32[]{:S(2)}) copy-start(f32[160,127]{1,0:T(8,128)} %points_hbm.1) | copy-start | bytes 243844
  52.9 0.9 %copy-start.2 = (f32[160,128]{1,0:T(8,128)S(1)}, f32[160,128]{1,0:T(8,128)}, u32[]{:S(2)}) copy-start(f32[160,128]{1,0:T(8,128)} %refs_6_.1) | copy-start | bytes 245764

commit v4 on v3

--- a/solution.py
+++ b/solution.py
@@ -376,14 +376,16 @@
                 work[hi:, 0:lo] -= e[:, 0:lo]
             work[hi:, lo:hi] = -e[:, lo:hi]
         after(p)
+        part = m_ref[lo:hi, :]
+        g = bdot(three_left(part.T), three_right(part, 0))
+        v.g[...] = g if p == 0 else v.g[...] + g
+        for s in ((0, 1), (2, 3), (4,), ())[p]:
+            rows = slice(2 * W * s, 2 * W * s + 2 * W)
+            v.own[rows, :] += bdot_nt(three_left(v.basis[rows, :]), v.l3[...])
 
 
 def prepare_rows(r, c, v):
-    for s in range(NR // 2):
-        rows = slice(2 * W * s, 2 * W * s + 2 * W)
-        v.own[rows, :] += bdot_nt(three_left(v.basis[rows, :]), v.l3[...])
-    g = bdot(three_left(v.m[...].T), three_right(v.m[...], 0))
-    g3 = three_right(g, 0)
+    g3 = three_right(v.g[...], 0)
     for s in range(NR // 2):
         rows = slice(2 * W * s, 2 * W * s + 2 * W)
         hs = bdot(three_left(v.own[rows, :]), g3)
@@ -420,9 +422,9 @@
 
 
 OUTS = (("square", (W, W), F32), ("table", (NT, 24, W), F32), ("h", (ROWS, LEAD + W), F32), ("lhs", (ROWS, 6 * W), BF),
-        ("panel", (ROWS, LEAD), F32))
-WORK = (("padded", (192, W), F32), ("lead", (LEAD, W), F32), ("noise", (8, W), F32), ("basis", (ROWS, W), F32),
-        ("m", (LEAD, LEAD), F32), ("work", (LEAD, LEAD), F32), ("own", (ROWS, LEAD), F32), ("kp", (ROWS, W), F32),
+        ("panel", (ROWS, LEAD), F32), ("noise", (NR * RG, W), F32))
+WORK = (("padded", (192, W), F32), ("lead", (LEAD, W), F32), ("basis", (ROWS, W), F32),
+        ("m", (LEAD, LEAD), F32), ("g", (LEAD, LEAD), F32), ("work", (LEAD, LEAD), F32), ("own", (ROWS, LEAD), F32), ("kp", (ROWS, W), F32),
         ("f3", (2 * W, 3 * LEAD), BF), ("l3", (LEAD, 3 * W), BF))
 
 
@@ -437,7 +439,7 @@
     moves = Moves(basis_hbm, v.lead, stage, cols_ref, sems)
     copies = [
         pltpu.make_async_copy(points_hbm, raw, in_sem.at[0]),
-        pltpu.make_async_copy(noise_hbm.at[pl.ds(0, 8)], v.noise, in_sem.at[1]),
+        pltpu.make_async_copy(noise_hbm, v.noise, in_sem.at[1]),
         pltpu.make_async_copy(basis_hbm, v.basis, in_sem.at[2]),
     ]
     for copy in copies:
@@ -453,9 +455,7 @@
     lead_products(v)
 
     def after(p):
-        if p < 2:
-            for n in range(CHUNKS // 2):
-                moves.forward(CHUNKS // 2 * p + n)
+        moves.forward(p)
 
     factor(v, after)
     prepare_rows(moves.r, moves.c, v)
@@ -485,10 +485,10 @@
             dma((2, 2, CHUNKS)),
         ],
         compiler_params=pltpu.CompilerParams(collective_id=0, has_side_effects=True, vmem_limit_bytes=32 << 20),
-    )(points, noise, basis)
-
-
-def finish_kernel(pos, square, table, h, lhs, panel, cols_ref, noise_ref, out_ref, rhs):
+    )(*[pltpu.with_memory_space_constraint(a, pltpu.HBM) for a in (points, noise, basis)])
+
+
+def finish_kernel(pos, square, table, h, lhs, panel, noise_ref, cols_ref, out_ref, rhs):
     r, c = pos()
     step = pl.program_id(0)
     same, _ = eye_masks()
@@ -541,7 +541,7 @@
                 out_ref[at, W * s:W * s + W] += jnp.where(same, noise_ref[pl.ds(NR * r + i, 1), :], 0.0)
 
 
-def finish_call(pos, prepared, noise):
+def finish_call(pos, prepared):
     full = pl.BlockSpec(memory_space=pltpu.VMEM)
     return pl.pallas_call(
         lambda *refs: finish_kernel(pos, *refs),
@@ -551,7 +551,7 @@
         out_specs=pl.BlockSpec((ROWS, 2 * W), lambda s: (0, s)),
         scratch_shapes=[pltpu.VMEM((6 * W, 2 * W), BF)],
         compiler_params=pltpu.CompilerParams(vmem_limit_bytes=32 << 20),
-    )(*prepared, noise)
+    )(*prepared)
 
 
 def body(points, noise, basis):
@@ -560,7 +560,7 @@
     def pos():
         return lax.axis_index("rows"), lax.axis_index("cols")
 
-    return finish_call(pos, prepared, noise)
+    return finish_call(pos, prepared)
 
 
 def solution(mesh):

time: 65.7 us -> 56 us (0.85)
  Pallas kernels: 61.7 us -> 55.8 us
  local copies, waits for them, and re-layouts: 3.74 us -> 0 us
    pallas_call x1, Pallas kernels: 50 us -> 44.1 us  [prepare(): pl.pallas_call(lead_kernel, out_shape=tuple((jax.ShapeDtypeStruct(o[1], o...]
    unnamed x8 -> x0, local copies, waits for them, and re-layouts: 3.74 us -> none
where the time goes in v4:
time: 56 us; the launch traced here: 55.8 us
  Pallas kernels  55.8 us (100%)
    pallas_call x1, Pallas kernels, prepare(): pl.pallas_call(lead_kernel, out_shape=tuple((jax.ShapeDtypeStruct(o[1], o...  44.1 us
    pallas_call x1, Pallas kernels, finish_call(): pl.pallas_call(lambda *refs: finish_kernel(pos, *refs), grid=(NC // 2,),...  11.7 us

profile of v4, /device:TPU:16, one launch (start us, length us, event | category | flops | bytes accessed | tf_op | source)
XLA Modules:
  0.0 55.8 jit_solution(4385411508714423507)
XLA Ops:
  0.0 44.1 %shard_map.37 = (f32[128,128]{1,0:T(8,128)S(1)}, f32[14,24,128]{2,1,0:T(8,128)S(1)}, f32[1280,640]{1,0:T(8,128)S(1)}, bf16[1280,768]{1,0:T(8,128)(2,1)S(1)}, f32...) custom-call(f32[160,127]{1,0:T(8,128)} %points_hbm.1, f32[160,128]{1,0:T(8,128)} %noise_hbm.1, ...), custom_call_target="tpu_custom_call" | custom-call | tf_op jit(solution)/shard_map/pallas_call | solution.py:468
  44.1 11.7 %shard_map.38 = f32[1280,2560]{1,0:T(8,128)} custom-call(f32[128,128]{1,0:T(8,128)S(1)} %get-tuple-element.12.refs_0_, f32[14,24,128]{2,1,0:T(8,128)S(1)} %get-tuple-element.13.refs_1_, f32[1280,640]{1,0:T(8,128)S(1)} %get-tuple-element.14.refs_2_, bf16[1280,768]{1,0:T(8,128)(2,1)S(1)} %get-tuple-element.15.refs_3_, ...), custom_call_target="tpu_custom_call" | custom-call | tf_op jit(solution)/shard_map/pallas_call | solution.py:546

commit v5 on v4

--- a/solution.py
+++ b/solution.py
@@ -303,10 +303,6 @@
     return lax.dot_general(a, b, (((1,), (0,)), ((), ())), preferred_element_type=F32)
 
 
-def bdot_nt(a, b):
-    return lax.dot_general(a, b, (((1,), (1,)), ((), ())), preferred_element_type=F32)
-
-
 def prepare_points(r, c, v):
     same, jmask = eye_masks()
     lane = lax.broadcasted_iota(jnp.int32, (W, W), 1)
@@ -334,7 +330,7 @@
         pieces = [q if n == m else jnp.zeros((24, W), F32) for n in range(NL)]
         coef.append(jnp.concatenate(pieces, axis=1))
     weights = jnp.concatenate([jnp.concatenate(total, axis=1)] + coef + [jnp.zeros((W - 24 * (NL + 1), LEAD), F32)], axis=0)
-    v.f3[0:W, :] = three_right(weights, 1)
+    v.f[0:W, :] = weights
     tc = pltpu.roll(t, W - COLS_AT, 1)
     for i in range(NR):
         a_row = square[ROWS_AT + i:ROWS_AT + i + 1, :]
@@ -377,34 +373,32 @@
             work[hi:, lo:hi] = -e[:, lo:hi]
         after(p)
         part = m_ref[lo:hi, :]
-        g = bdot(three_left(part.T), three_right(part, 0))
+        g = dot_tn(part, part)
         v.g[...] = g if p == 0 else v.g[...] + g
         for s in ((0, 1), (2, 3), (4,), ())[p]:
             rows = slice(2 * W * s, 2 * W * s + 2 * W)
-            v.own[rows, :] += bdot_nt(three_left(v.basis[rows, :]), v.l3[...])
+            v.own[rows, :] += dot_nt(v.basis[rows, :], v.lead[...])
 
 
 def prepare_rows(r, c, v):
-    g3 = three_right(v.g[...], 0)
     for s in range(NR // 2):
         rows = slice(2 * W * s, 2 * W * s + 2 * W)
-        hs = bdot(three_left(v.own[rows, :]), g3)
+        hs = dot(v.own[rows, :], v.g[...])
         b = v.basis[rows, :]
         if s < NL // 2:
             hs = jnp.where(r == 0, -v.m[rows, :], hs)
             b = jnp.where(r == 0, 0.0, b)
         for m in range(NL):
             v.h[rows, W * m:W * m + W] = jnp.where(lax.broadcasted_iota(jnp.int32, (2 * W, W), 1) > 0, hs[:, W * m:W * m + W], 0.0)
-        eb = bdot_nt(three_left(hs), v.f3[...])
+        eb = dot_nt(hs, v.f[...])
         v.lhs[rows, 0:3 * W] = three_left(b - eb[:, W:])
         v.lhs[rows, 3 * W:] = three_left(eb[:, 0:W] + v.kp[rows, :])
 
     @pl.when(c == 0)
     def _():
-        m3 = three_left(v.m[...])
         for s in range(NR // 2):
             rows = slice(2 * W * s, 2 * W * s + 2 * W)
-            x = bdot_nt(three_right(v.own[rows, :], 1), m3)
+            x = dot_nt(v.own[rows, :], v.m[...])
             rid = 2 * W * s + lax.broadcasted_iota(jnp.int32, (2 * W, LEAD), 0)
             cid = lax.broadcasted_iota(jnp.int32, (2 * W, LEAD), 1)
             v.panel[rows, :] = jnp.where((r == 0) & (rid < cid), 0.0, x)
@@ -417,15 +411,14 @@
 
 
 def lead_products(v):
-    v.l3[...] = three_right(v.lead[...], 1)
-    v.f3[W:2 * W, :] = three_right(v.lead[...].T, 1)
+    v.f[W:2 * W, :] = v.lead[...].T
 
 
 OUTS = (("square", (W, W), F32), ("table", (NT, 24, W), F32), ("h", (ROWS, LEAD + W), F32), ("lhs", (ROWS, 6 * W), BF),
         ("panel", (ROWS, LEAD), F32), ("noise", (NR * RG, W), F32))
 WORK = (("padded", (192, W), F32), ("lead", (LEAD, W), F32), ("basis", (ROWS, W), F32),
         ("m", (LEAD, LEAD), F32), ("g", (LEAD, LEAD), F32), ("work", (LEAD, LEAD), F32), ("own", (ROWS, LEAD), F32), ("kp", (ROWS, W), F32),
-        ("f3", (2 * W, 3 * LEAD), BF), ("l3", (LEAD, 3 * W), BF))
+        ("f", (2 * W, LEAD), F32))
 
 
 def lead_kernel(points_hbm, noise_hbm, basis_hbm, *refs):

time: 56 us -> 60.3 us (1.077)
  Pallas kernels: 55.8 us -> 60.1 us
    pallas_call x1, Pallas kernels: 44.1 us -> 48.4 us  [prepare(): pl.pallas_call(lead_kernel, out_shape=tuple((jax.ShapeDtypeStruct(o[1], o...]
where the time goes in v5:
time: 60.3 us; the launch traced here: 60.1 us
  Pallas kernels  60.1 us (100%)
    pallas_call x1, Pallas kernels, prepare(): pl.pallas_call(lead_kernel, out_shape=tuple((jax.ShapeDtypeStruct(o[1], o...  48.4 us
    pallas_call x1, Pallas kernels, finish_call(): pl.pallas_call(lambda *refs: finish_kernel(pos, *refs), grid=(NC // 2,),...  11.7 us

profile of v5, /device:TPU:16, one launch (start us, length us, event | category | flops | bytes accessed | tf_op | source)
XLA Modules:
  0.0 60.1 jit_solution(8064419659806331953)
XLA Ops:
  0.0 48.4 %shard_map.37 = (f32[128,128]{1,0:T(8,128)S(1)}, f32[14,24,128]{2,1,0:T(8,128)S(1)}, f32[1280,640]{1,0:T(8,128)S(1)}, bf16[1280,768]{1,0:T(8,128)(2,1)S(1)}, f32...) custom-call(f32[160,127]{1,0:T(8,128)} %points_hbm.1, f32[160,128]{1,0:T(8,128)} %noise_hbm.1, ...), custom_call_target="tpu_custom_call" | custom-call | tf_op jit(solution)/shard_map/pallas_call | solution.py:461
  48.4 11.7 %shard_map.38 = f32[1280,2560]{1,0:T(8,128)} custom-call(f32[128,128]{1,0:T(8,128)S(1)} %get-tuple-element.12.refs_0_, f32[14,24,128]{2,1,0:T(8,128)S(1)} %get-tuple-element.13.refs_1_, f32[1280,640]{1,0:T(8,128)S(1)} %get-tuple-element.14.refs_2_, bf16[1280,768]{1,0:T(8,128)(2,1)S(1)} %get-tuple-element.15.refs_3_, ...), custom_call_target="tpu_custom_call" | custom-call | tf_op jit(solution)/shard_map/pallas_call | solution.py:539

commit v6 on v5

--- a/solution.py
+++ b/solution.py
@@ -398,7 +398,10 @@
     def _():
         for s in range(NR // 2):
             rows = slice(2 * W * s, 2 * W * s + 2 * W)
-            x = dot_nt(v.own[rows, :], v.m[...])
+            x = jnp.concatenate([
+                dot_nt(v.own[rows, 0:2 * W], v.m[0:2 * W, 0:2 * W]),
+                dot_nt(v.own[rows, :], v.m[2 * W:, :]),
+            ], axis=1)
             rid = 2 * W * s + lax.broadcasted_iota(jnp.int32, (2 * W, LEAD), 0)
             cid = lax.broadcasted_iota(jnp.int32, (2 * W, LEAD), 1)
             v.panel[rows, :] = jnp.where((r == 0) & (rid < cid), 0.0, x)

time: 60.3 us -> 60 us (level)
  no operation moved by 1% of the time
where the time goes in v6:
time: 60 us; the launch traced here: 59.9 us
  Pallas kernels  59.8 us (100%)
    pallas_call x1, Pallas kernels, prepare(): pl.pallas_call(lead_kernel, out_shape=tuple((jax.ShapeDtypeStruct(o[1], o...  48.1 us
    pallas_call x1, Pallas kernels, finish_call(): pl.pallas_call(lambda *refs: finish_kernel(pos, *refs), grid=(NC // 2,),...  11.7 us

profile of v6, /device:TPU:16, one launch (start us, length us, event | category | flops | bytes accessed | tf_op | source)
XLA Modules:
  0.0 59.9 jit_solution(13322394062671537302)
XLA Ops:
  0.0 48.1 %shard_map.37 = (f32[128,128]{1,0:T(8,128)S(1)}, f32[14,24,128]{2,1,0:T(8,128)S(1)}, f32[1280,640]{1,0:T(8,128)S(1)}, bf16[1280,768]{1,0:T(8,128)(2,1)S(1)}, f32...) custom-call(f32[160,127]{1,0:T(8,128)} %points_hbm.1, f32[160,128]{1,0:T(8,128)} %noise_hbm.1, ...), custom_call_target="tpu_custom_call" | custom-call | tf_op jit(solution)/shard_map/pallas_call | solution.py:464
  48.2 11.7 %shard_map.38 = f32[1280,2560]{1,0:T(8,128)} custom-call(f32[128,128]{1,0:T(8,128)S(1)} %get-tuple-element.12.refs_0_, f32[14,24,128]{2,1,0:T(8,128)S(1)} %get-tuple-element.13.refs_1_, f32[1280,640]{1,0:T(8,128)S(1)} %get-tuple-element.14.refs_2_, bf16[1280,768]{1,0:T(8,128)(2,1)S(1)} %get-tuple-element.15.refs_3_, ...), custom_call_target="tpu_custom_call" | custom-call | tf_op jit(solution)/shard_map/pallas_call | solution.py:542
